TPU v7x, 512 devices: a whole 4x8x8 slice. The times are simulated.
512 devices in a mesh: seq: 16 (over x_hi, y), fsdp: 16 (over z, core), dp: 2 (over x_lo).
Axes of the slice: x: 4 (x_hi: 2, x_lo: 2; x = x_hi * 2 + x_lo), y: 8, z: 8, core: 2. Of those that a mesh axis runs over, the one named last changes fastest.
Arguments:
- query_rows: bfloat16 [16, 2048, 2048], P('fsdp', 'seq', 'dp'), may hold values from -32 to 32
- key_rows: bfloat16 [16, 2048, 2048], P('fsdp', 'seq', 'dp'), may hold values from -32 to 32
- value_rows: bfloat16 [16, 2048, 2048], P('fsdp', 'seq', 'dp'), may hold values from -6 to 6
- summary_keys: bfloat16 [16, 128, 2048], P('fsdp', 'seq', 'dp'), may hold values from -6 to 6
- summary_values: bfloat16 [16, 128, 2048], P('fsdp', 'seq', 'dp'), may hold values from -6 to 6
- out_grad: bfloat16 [16, 2048, 2048], P('fsdp', 'seq', 'dp'), may hold values from -6 to 6
- rel_bias: float32 [4, 16], P(None, 'fsdp'), may hold values from -2 to 2
- pattern: int32 [16, 16, 3], P('fsdp'), may hold values from -1 to 15, as said below
- block_view: int32 [16, 16], P('fsdp'), may hold values from 0 to 95, as said below
- summary_view: int32 [16, 128], P('fsdp'), may hold values from 0 to 95
Outputs:
- attended: bfloat16 [16, 2048, 2048], P('fsdp', 'seq', 'dp')
- query_grad: bfloat16 [16, 2048, 2048], P('fsdp', 'seq', 'dp')
- key_grad: bfloat16 [16, 2048, 2048], P('fsdp', 'seq', 'dp')
- value_grad: bfloat16 [16, 2048, 2048], P('fsdp', 'seq', 'dp')
- summary_key_grad: bfloat16 [16, 128, 2048], P('fsdp', 'seq', 'dp')
- summary_value_grad: bfloat16 [16, 128, 2048], P('fsdp', 'seq', 'dp')
- bias_grad: float32 [4, 16], P(None, 'fsdp')
Inputs may be any that keep to these rules, and one draw needn't show every extreme that they name: `pattern`: slot j of block b's list holds b + j - 1 or -1 (no block); slot 1 always holds b. `block_view`: blocks that follow each other have equal views or views one apart on the cycle of 96 views.
All inputs are finite; a program needn't handle non-finite values.
Results may differ from a plain program's by a relative error of at most 0.0074.
Values may be sent and summed in bfloat16 or wider, within the bound.
No kernel may reach another device: no remote copies, remote signals or barrier semaphores. Data moves between devices by JAX's collectives and lax.ppermute only.
A program may use at most 64 MiB of HBM per device.

v0:
```python
import functools
import math

import jax
import jax.numpy as jnp
from jax import lax
from jax.experimental import pallas as pl
from jax.experimental.pallas import tpu as pltpu
from jax.sharding import PartitionSpec as P


HSIZE = 128
BLK = 128
NVIEW = 96
NREL = 4
NEG_FILL = -1e30
SCALE = 1.0 / math.sqrt(HSIZE)


def view_class(view_a, view_b):
    distance = jnp.abs(view_a - view_b)
    distance = jnp.minimum(distance, NVIEW - distance)
    one = jnp.int32(1)
    zero = jnp.int32(0)
    return (
        jnp.where(distance >= 1, one, zero)
        + jnp.where(distance >= 2, one, zero)
        + jnp.where(distance >= 8, one, zero)
    )


def dot_nt(left, right):
    return lax.dot_general(left, right, (((1,), (1,)), ((), ())), preferred_element_type=jnp.float32)


def dot_nn(left, right):
    return lax.dot_general(left, right, (((1,), (0,)), ((), ())), preferred_element_type=jnp.float32)


def dot_tn(left, right):
    return lax.dot_general(left, right, (((0,), (0,)), ((), ())), preferred_element_type=jnp.float32)


def attention_kernel(
    heads,
    nblk,
    ndp,
    place,
    pattern,
    views,
    table,
    sum_views,
    query,
    grad_out,
    own_kv,
    left_kv,
    right_kv,
    sums,
    attended,
    query_grad,
    to_left,
    to_right,
    own_grad,
    sum_grad,
    bias_part,
):
    block = place[0]
    head_start = place[1]
    own_view = views[block]
    slot_views = [
        views[jnp.maximum(block - 1, 0)],
        own_view,
        views[jnp.minimum(block + 1, nblk - 1)],
    ]
    slot_class = [view_class(own_view, view) for view in slot_views]
    slot_mask = [
        jnp.where(pattern[block, slot] >= 0, jnp.float32(0.0), jnp.float32(NEG_FILL))
        for slot in range(3)
    ]
    sum_class = view_class(own_view, sum_views[...])
    count, rows = sums.shape[0], sums.shape[1] // 2
    bias_part[...] = jnp.zeros_like(bias_part)
    ride = heads * HSIZE
    sum_grad[:, :, ride:] = jnp.zeros((count, 2 * rows, BLK), jnp.bfloat16)
    class_row = lax.broadcasted_iota(jnp.int32, (8, BLK), 0)
    class_lane = lax.broadcasted_iota(jnp.int32, (8, BLK), 1)
    for head in range(heads):
        cols = slice(head * HSIZE, (head + 1) * HSIZE)
        q = query[:, cols]
        go = grad_out[:, cols]
        keys = jnp.concatenate(
            [
                left_kv[0, :, cols],
                own_kv[0, :, cols],
                right_kv[0, :, cols],
                sums[:, :rows, cols].reshape(count * rows, HSIZE),
            ],
            axis=0,
        )
        values = jnp.concatenate(
            [
                left_kv[1, :, cols],
                own_kv[1, :, cols],
                right_kv[1, :, cols],
                sums[:, rows:, cols].reshape(count * rows, HSIZE),
            ],
            axis=0,
        )
        biases = [table[c, head_start + head] for c in range(NREL)]

        def pick(cls):
            low = jnp.where(cls == 0, biases[0], biases[1])
            high = jnp.where(cls == 2, biases[2], biases[3])
            return jnp.where(cls < 2, low, high)

        raw = dot_nt(keys, q) * SCALE
        scores = jnp.concatenate(
            [
                raw[slot * BLK : (slot + 1) * BLK] + (pick(slot_class[slot]) + slot_mask[slot])
                for slot in range(3)
            ]
            + [raw[3 * BLK :] + pick(sum_class)],
            axis=0,
        )
        row_max = jnp.max(scores, axis=0, keepdims=True)
        lifted = jnp.exp(scores - row_max)
        weights = lifted * (1.0 / jnp.sum(lifted, axis=0, keepdims=True))
        low = weights.astype(jnp.bfloat16)
        prob_grad = dot_nt(values, go)
        row_delta = jnp.sum(weights * prob_grad, axis=0, keepdims=True)
        score_grad = weights * (prob_grad - row_delta)
        grad_low = score_grad.astype(jnp.bfloat16)
        attended[:, cols] = dot_tn(low, values).astype(jnp.bfloat16)
        query_grad[:, cols] = (dot_tn(grad_low, keys) * SCALE).astype(jnp.bfloat16)
        key_terms = dot_nn(grad_low, q)
        value_terms = dot_nn(low, go)
        for index, terms in enumerate((key_terms, value_terms)):
            to_left[index, :, cols] = terms[:BLK].astype(jnp.bfloat16)
            own_grad[index, :, cols] = terms[BLK : 2 * BLK]
            to_right[index, :, cols] = terms[2 * BLK : 3 * BLK].astype(jnp.bfloat16)
            sum_grad[:, index * rows : (index + 1) * rows, cols] = (
                terms[3 * BLK :].astype(jnp.bfloat16).reshape(count, rows, HSIZE)
            )
        slot_sums = [
            jnp.sum(score_grad[slot * BLK : (slot + 1) * BLK], axis=0, keepdims=True)
            for slot in range(3)
        ]
        sum_part = score_grad[3 * BLK :]
        tile = jnp.zeros((8, BLK), jnp.float32)
        for c in range(NREL):
            line = jnp.sum(jnp.where(sum_class == c, sum_part, 0.0), axis=0, keepdims=True)
            for slot in range(3):
                line = line + jnp.where(slot_class[slot] == c, slot_sums[slot], 0.0)
            tile = jnp.where(class_row == c, line, tile)
        totals = jnp.where(class_row == class_lane, jnp.sum(tile, axis=1, keepdims=True), 0.0)
        line = jnp.sum(totals, axis=0, keepdims=True)
        for copy in range(ndp):
            bias_part[ndp * (head_start + head) + copy] = line


def body(
    query_rows,
    key_rows,
    value_rows,
    summary_keys,
    summary_values,
    out_grad,
    rel_bias,
    pattern,
    block_view,
    summary_view,
):
    tok_rows, width = query_rows.shape[1:]
    heads = width // HSIZE
    nseq = lax.axis_size("seq")
    nfsdp = lax.axis_size("fsdp")
    ndp = lax.axis_size("dp")
    nblk = block_view.shape[1]
    sum_rows = summary_keys.shape[1]
    bf16, f32 = jnp.bfloat16, jnp.float32

    up = [(i, i + 1) for i in range(nseq - 1)]
    down = [(i + 1, i) for i in range(nseq - 1)]
    own_kv = jnp.stack([key_rows[0], value_rows[0]])
    left_kv = lax.ppermute(own_kv, "seq", up)
    right_kv = lax.ppermute(own_kv, "seq", down)
    own_sums = jnp.concatenate([summary_keys[0], summary_values[0]], axis=0)
    sums_out = jnp.broadcast_to(own_sums[None], (nseq, 2 * sum_rows, width))
    sums = lax.all_to_all(sums_out, "seq", 0, 0, tiled=True)
    table = lax.all_gather(rel_bias, "fsdp", axis=1, tiled=True)
    place = jnp.stack([lax.axis_index("seq"), lax.axis_index("dp") * heads]).astype(jnp.int32)

    smem = pl.BlockSpec(memory_space=pltpu.SMEM)
    vmem = pl.BlockSpec(memory_space=pltpu.VMEM)
    shaped = jax.ShapeDtypeStruct
    attended, query_grad, to_left, to_right, own_grad, sum_grad, bias_part = pl.pallas_call(
        functools.partial(attention_kernel, heads, nblk, ndp),
        out_shape=(
            shaped((tok_rows, width), bf16),
            shaped((tok_rows, width), bf16),
            shaped((2, BLK, width), bf16),
            shaped((2, BLK, width), bf16),
            shaped((2, BLK, width), f32),
            shaped((nseq, 2 * sum_rows, width + BLK), bf16),
            shaped((nfsdp * ndp, 1, BLK), f32),
        ),
        in_specs=[smem] * 4 + [vmem] * 7,
        out_specs=(vmem,) * 7,
        name="attention",
    )(
        place,
        pattern[0],
        block_view[0],
        table,
        summary_view.reshape(-1, 1),
        query_rows[0],
        out_grad[0],
        own_kv,
        left_kv,
        right_kv,
        sums,
    )
    from_right = lax.ppermute(to_left, "seq", down)
    from_left = lax.ppermute(to_right, "seq", up)
    bias_part = lax.all_to_all(bias_part, ("fsdp", "dp"), 0, 0, tiled=True)
    rest = jnp.sum(bias_part, axis=0)
    pieces = []
    for _ in range(3):
        pieces.append(lax.reduce_precision(rest, 8, 7))
        rest = rest - pieces[-1]
    rider = jnp.pad(jnp.concatenate(pieces, axis=0).astype(bf16), ((0, 2 * sum_rows - 3), (0, 0)))
    rider = jnp.broadcast_to(rider[None], (nseq, 2 * sum_rows, BLK))
    sum_grad = lax.dynamic_update_slice(sum_grad, rider, (0, 0, width))
    sum_terms = lax.all_to_all(sum_grad, "seq", 0, 0, tiled=True)

    grads = own_grad + from_left.astype(f32) + from_right.astype(f32)
    key_grad = (grads[0] * SCALE).astype(bf16)
    value_grad = grads[1].astype(bf16)
    summary = jnp.sum(sum_terms.astype(f32), axis=0)
    summary_key_grad = (summary[:sum_rows, :width] * SCALE).astype(bf16)
    summary_value_grad = summary[sum_rows:, :width].astype(bf16)
    bias_grad = jnp.sum(summary[:3, width : width + NREL], axis=0).reshape(NREL, 1)
    return (
        attended[None],
        query_grad[None],
        key_grad[None],
        value_grad[None],
        summary_key_grad[None],
        summary_value_grad[None],
        bias_grad,
    )


def solution(mesh):
    rows = P("fsdp", "seq", "dp")
    return jax.shard_map(
        body,
        mesh=mesh,
        in_specs=(rows,) * 6
        + (P(None, "fsdp"), P("fsdp", None, None), P("fsdp", None), P("fsdp", None)),
        out_specs=(rows,) * 6 + (P(None, "fsdp"),),
        check_vma=False,
    )
```

profile of v0, /device:TPU:4, one launch (start us, length us, event | category | flops | bytes accessed | tf_op | source)
XLA Modules:
  0.0 106.4 jit_solution(2693828458963390197)
XLA Ops:
  0.6 0.0 copy-start.5
  0.6 0.8 pad_maximum_fusion
  1.4 0.0 copy-start.6
  1.4 0.8 broadcast_in_dim.12
  2.3 0.0 copy-start.9
  2.3 0.0 copy-start.7
  2.3 0.0 copy-start.8
  2.3 10.2 %all-to-all-start = ((bf16[16,16,1024]{2,1,0:T(8,128)(2,1)}), bf16[16,16,1024]{2,1,0:T(8,128)(2,1)S(1)}, u32[]{:S(2)}, u32[]{:S(2)}) async-start(bf16[16,16,1024]{2,1,0:T(8,128)(2,1)} %broadcast_in_dim.12), calls=%async_computation | async-start | bytes 1048576 | tf_op jit(solution)/shard_map/all_to_all | solution.py:189
  12.5 0.0 copy-done.5
  12.5 0.0 copy-done.6
  12.6 0.0 copy-start.1
  12.6 4.6 %collective-permute-start.1 = (bf16[2,128,1024]{2,1,0:T(8,128)(2,1)S(1)}, bf16[2,128,1024]{2,1,0:T(8,128)(2,1)S(1)}, u32[]{:S(2)}, u32[]{:S(2)}) collective-permute-start(bf16[2,128,1024]{2,1,0:T(8,128)(2,1)S(1)} %constant_dynamic-update-slice_fusion.own_kv), channel_id=1, source_target_pairs={{32,0},{64,32},{96,64},{128,96},{160,128},{192,160},{224,192},{256... | collective-permute-start | bytes 1572872 | tf_op jit(solution)/shard_map/ppermute | solution.py:186
  17.2 1.9 %collective-permute-start = (bf16[2,128,1024]{2,1,0:T(8,128)(2,1)S(1)}, bf16[2,128,1024]{2,1,0:T(8,128)(2,1)S(1)}, u32[]{:S(2)}, u32[]{:S(2)}) collective-permute-start(bf16[2,128,1024]{2,1,0:T(8,128)(2,1)S(1)} %constant_dynamic-update-slice_fusion.own_kv), channel_id=1, source_target_pairs={{0,32},{32,64},{64,96},{96,128},{128,160},{160,192},{192,224},{224... | collective-permute-start | bytes 1572872 | tf_op jit(solution)/shard_map/ppermute | solution.py:185
  19.1 0.0 copy-done.9
  19.1 23.2 %all-gather = f32[16,1,4]{2,1,0:T(1,128)S(1)} all-gather(f32[1,1,4]{2,1,0:T(1,128)S(1)} %bitcast.34), channel_id=1, replica_groups=mesh['seq'=16,'fsdp'=16,'dp'=2] {'fsdp'}, dimensions={0}, use_global_device_ids=true | all-gather | bytes 272 | tf_op jit(solution)/shard_map/all_gather | solution.py:190
  42.3 0.7 copy.20
  42.9 0.0 copy-done.7
  42.9 0.7 copy.23
  43.6 0.0 copy-done.8
  43.6 0.7 copy.22.sum_views
  44.4 0.6 pad_add_fusion.place
  44.9 0.0 collective-permute-done.1.right_kv
  44.9 0.0 collective-permute-done.left_kv
  45.0 0.0 copy-start.4
  45.0 0.0 all-to-all-done.sums
  45.0 0.0 copy-start
  45.0 0.0 copy-done.1
  45.0 0.8 copy-done.3
  45.8 0.2 copy-done.4
  45.9 0.2 copy-done
  46.1 8.0 %attention.1 = (bf16[128,1024]{1,0:T(8,128)(2,1)}, bf16[128,1024]{1,0:T(8,128)(2,1)}, bf16[2,128,1024]{2,1,0:T(8,128)(2,1)}, bf16[2,128,1024]{2,1,0:T(8,128)(2,1...) custom-call(s32[2]{0:T(128)} %pad_add_fusion.place, s32[16,3]{1,0:T(8,128)} %bitcast.29, ...), custom_call_target="tpu_custom_call" | custom-call | tf_op jit(solution)/shard_map/attention/pallas_call | solution.py:196
  54.1 12.5 %all_to_all.15 = f32[32,1,128]{2,1,0:T(1,128)S(1)} all-to-all(f32[32,1,128]{2,1,0:T(1,128)} %get-tuple-element.20), channel_id=1, replica_groups=mesh['seq'=16,'fsdp'=16,'dp'=2] {'fsdp','dp'}, dimensions={0} | all-to-all | bytes 32768 | tf_op jit(solution)/shard_map/all_to_all | solution.py:225
  66.7 0.1 reduce_sum.29
  66.8 0.7 broadcast_dynamic-update-slice_fusion
  67.4 8.6 %all-to-all-start.2 = ((bf16[16,16,1152]{2,1,0:T(8,128)(2,1)}), bf16[16,16,1152]{2,1,0:T(8,128)(2,1)S(1)}, u32[]{:S(2)}, u32[]{:S(2)}) async-start(bf16[16,16,1152]{2,1,0:T(8,128)(2,1)} %broadcast_dynamic-update-slice_fusion), calls=%async_computation.2 | async-start | bytes 1179648 | tf_op jit(solution)/shard_map/all_to_all | solution.py:234
  76.0 3.4 %collective-permute-start.2 = (bf16[2,128,1024]{2,1,0:T(8,128)(2,1)}, bf16[2,128,1024]{2,1,0:T(8,128)(2,1)S(1)}, u32[]{:S(2)}, u32[]{:S(2)}) collective-permute-start(bf16[2,128,1024]{2,1,0:T(8,128)(2,1)} %get-tuple-element.17), channel_id=1, source_target_pairs={{0,32},{32,64},{64,96},{96,128},{128,160},{160,192},{192,224},{224... | collective-permute-start | bytes 1572872 | tf_op jit(solution)/shard_map/ppermute | solution.py:224
  79.4 6.1 %collective-permute-start.3 = (bf16[2,128,1024]{2,1,0:T(8,128)(2,1)}, bf16[2,128,1024]{2,1,0:T(8,128)(2,1)S(1)}, u32[]{:S(2)}, u32[]{:S(2)}) collective-permute-start(bf16[2,128,1024]{2,1,0:T(8,128)(2,1)} %get-tuple-element.18), channel_id=1, source_target_pairs={{32,0},{64,32},{96,64},{128,96},{160,128},{192,160},{224,192},{256... | collective-permute-start | bytes 1572872 | tf_op jit(solution)/shard_map/ppermute | solution.py:223
  85.5 17.3 %collective-permute-done.2 = bf16[2,128,1024]{2,1,0:T(8,128)(2,1)S(1)} collective-permute-done((bf16[2,128,1024]{2,1,0:T(8,128)(2,1)}, bf16[2,128,1024]{2,1,0:T(8,128)(2,1)S(1)}, u32[]{:S(2)}, u32[]{:S(2)}) %collective-permute-start.2) | collective-permute-done | bytes 524320 | tf_op jit(solution)/shard_map/ppermute | solution.py:224
  102.8 0.0 collective-permute-done.3
  102.8 0.0 copy-done.2
  102.8 0.2 convert_add_fusion
  103.1 0.7 slice.40
  103.8 0.8 fusion
  104.6 0.0 all-to-all-done.2
  104.6 0.1 convert_reduce_fusion
  104.7 0.5 slice_reduce_fusion
  105.2 0.6 fusion.3
  105.8 0.6 fusion.2
  (6 shorter events, 0.1 us)
Async XLA Ops:
  0.6 11.9 %copy-start.5 = (bf16[1,128,1024]{2,1,0:T(8,128)(2,1)S(1)}, bf16[1,128,1024]{2,1,0:T(8,128)(2,1)}, u32[]{:S(2)}) copy-start(bf16[1,128,1024]{2,1,0:T(8,128)(2,1)} %param.11) | copy-start | bytes 786436
  1.4 11.1 %copy-start.6 = (bf16[1,128,1024]{2,1,0:T(8,128)(2,1)S(1)}, bf16[1,128,1024]{2,1,0:T(8,128)(2,1)}, u32[]{:S(2)}) copy-start(bf16[1,128,1024]{2,1,0:T(8,128)(2,1)} %param.12) | copy-start | bytes 786436
  2.3 16.8 %copy-start.9 = (f32[4,1]{0,1:T(1,128)S(1)}, f32[4,1]{0,1:T(1,128)}, u32[]{:S(2)}) copy-start(f32[4,1]{0,1:T(1,128)} %param.16) | copy-start | bytes 52
  2.3 40.7 %copy-start.7 = (s32[1,16,3]{1,0,2:T(1,128)S(1)}, s32[1,16,3]{1,0,2:T(1,128)}, u32[]{:S(2)}) copy-start(s32[1,16,3]{1,0,2:T(1,128)} %param.17) | copy-start | bytes 580
  2.3 41.3 %copy-start.8 = (s32[1,128]{1,0:T(1,128)S(1)}, s32[1,128]{1,0:T(1,128)}, u32[]{:S(2)}) copy-start(s32[1,128]{1,0:T(1,128)} %param.19) | copy-start | bytes 1540
  2.3 42.7 %all-to-all-start = ((bf16[16,16,1024]{2,1,0:T(8,128)(2,1)}), bf16[16,16,1024]{2,1,0:T(8,128)(2,1)S(1)}, u32[]{:S(2)}, u32[]{:S(2)}) async-start(bf16[16,16,1024]{2,1,0:T(8,128)(2,1)} %broadcast_in_dim.12), calls=%async_computation | async-start | bytes 1048576 | tf_op jit(solution)/shard_map/all_to_all | solution.py:189
  12.6 32.4 %copy-start.1 = (bf16[2,128,1024]{2,1,0:T(8,128)(2,1)}, bf16[2,128,1024]{2,1,0:T(8,128)(2,1)S(1)}, u32[]{:S(2)}) copy-start(bf16[2,128,1024]{2,1,0:T(8,128)(2,1)S(1)} %constant_dynamic-update-slice_fusion.own_kv) | copy-start | bytes 1572868
  12.6 32.4 %collective-permute-start.1 = (bf16[2,128,1024]{2,1,0:T(8,128)(2,1)S(1)}, bf16[2,128,1024]{2,1,0:T(8,128)(2,1)S(1)}, u32[]{:S(2)}, u32[]{:S(2)}) collective-permute-start(bf16[2,128,1024]{2,1,0:T(8,128)(2,1)S(1)} %constant_dynamic-update-slice_fusion.own_kv), channel_id=1, source_target_pairs={{32,0},{64,32},{96,64},{128,96},{160,128},{192,160},{224,192},{256... | collective-permute-start | bytes 1572872 | tf_op jit(solution)/shard_map/ppermute | solution.py:186
  17.2 27.8 %collective-permute-start = (bf16[2,128,1024]{2,1,0:T(8,128)(2,1)S(1)}, bf16[2,128,1024]{2,1,0:T(8,128)(2,1)S(1)}, u32[]{:S(2)}, u32[]{:S(2)}) collective-permute-start(bf16[2,128,1024]{2,1,0:T(8,128)(2,1)S(1)} %constant_dynamic-update-slice_fusion.own_kv), channel_id=1, source_target_pairs={{0,32},{32,64},{64,96},{96,128},{128,160},{160,192},{192,224},{224... | collective-permute-start | bytes 1572872 | tf_op jit(solution)/shard_map/ppermute | solution.py:185
  44.9 0.8 copy-start.3
  45.0 1.0 copy-start.4
  45.0 1.1 %copy-start = (bf16[16,16,1024]{2,1,0:T(8,128)(2,1)}, bf16[16,16,1024]{2,1,0:T(8,128)(2,1)S(1)}, u32[]{:S(2)}) copy-start(bf16[16,16,1024]{2,1,0:T(8,128)(2,1)S(1)} %all-to-all-done.sums) | copy-start | bytes 1572868
  54.1 48.7 %copy-start.2 = (f32[2,128,1024]{2,1,0:T(8,128)S(1)}, f32[2,128,1024]{2,1,0:T(8,128)}, u32[]{:S(2)}) copy-start(f32[2,128,1024]{2,1,0:T(8,128)} %get-tuple-element.16) | copy-start | bytes 3145732
  67.4 37.2 %all-to-all-start.2 = ((bf16[16,16,1152]{2,1,0:T(8,128)(2,1)}), bf16[16,16,1152]{2,1,0:T(8,128)(2,1)S(1)}, u32[]{:S(2)}, u32[]{:S(2)}) async-start(bf16[16,16,1152]{2,1,0:T(8,128)(2,1)} %broadcast_dynamic-update-slice_fusion), calls=%async_computation.2 | async-start | bytes 1179648 | tf_op jit(solution)/shard_map/all_to_all | solution.py:234
  76.0 26.8 %collective-permute-start.2 = (bf16[2,128,1024]{2,1,0:T(8,128)(2,1)}, bf16[2,128,1024]{2,1,0:T(8,128)(2,1)S(1)}, u32[]{:S(2)}, u32[]{:S(2)}) collective-permute-start(bf16[2,128,1024]{2,1,0:T(8,128)(2,1)} %get-tuple-element.17), channel_id=1, source_target_pairs={{0,32},{32,64},{64,96},{96,128},{128,160},{160,192},{192,224},{224... | collective-permute-start | bytes 1572872 | tf_op jit(solution)/shard_map/ppermute | solution.py:224
  79.4 23.4 %collective-permute-start.3 = (bf16[2,128,1024]{2,1,0:T(8,128)(2,1)}, bf16[2,128,1024]{2,1,0:T(8,128)(2,1)S(1)}, u32[]{:S(2)}, u32[]{:S(2)}) collective-permute-start(bf16[2,128,1024]{2,1,0:T(8,128)(2,1)} %get-tuple-element.18), channel_id=1, source_target_pairs={{32,0},{64,32},{96,64},{128,96},{160,128},{192,160},{224,192},{256... | collective-permute-start | bytes 1572872 | tf_op jit(solution)/shard_map/ppermute | solution.py:223
where the time goes:
time: 107 us; the launch traced here: 106 us
  blocking collectives  35.7 us (33%)
  starting transfers between devices  34.8 us (33%)
  waiting for transfers between devices  17.4 us (16%)
  Pallas kernels  8.03 us (8%)
  local copies, waits for them, and re-layouts  6.11 us (6%)
  other arithmetic  3.66 us (3%)
    all_gather x1, blocking collectives, body(): table = lax.all_gather(rel_bias, 'fsdp', axis=1, tiled=True)  23.2 us
    ppermute x1, waiting for transfers between devices, body(): from_left = lax.ppermute(to_right, 'seq', up)  17.3 us
    all_to_all x1, blocking collectives, body(): bias_part = lax.all_to_all(bias_part, ('fsdp', 'dp'), 0, 0, tiled=True)  12.5 us
    all_to_all x1, starting transfers between devices, body(): sums = lax.all_to_all(sums_out, 'seq', 0, 0, tiled=True)  10.2 us
    all_to_all x1, starting transfers between devices, body(): sum_terms = lax.all_to_all(sum_grad, 'seq', 0, 0, tiled=True)  8.61 us
    pallas_call x1, Pallas kernels, body(): pl.pallas_call(functools.partial(attention_kernel, heads, nblk, ndp), out...  8.03 us
    ppermute x1, starting transfers between devices, body(): from_right = lax.ppermute(to_left, 'seq', down)  6.08 us
    ppermute x1, starting transfers between devices, body(): right_kv = lax.ppermute(own_kv, 'seq', down)  4.58 us
  transfers between devices with their start and end apart: 6, of which 1 were waited for; matrix products, arithmetic and copies ran while one was open for 4% of the time, Pallas kernels for 0%

commit v1 on v0

--- a/solution.py
+++ b/solution.py
@@ -13,6 +13,7 @@
 BLK = 128
 NVIEW = 96
 NREL = 4
+RIDE = 8
 NEG_FILL = -1e30
 SCALE = 1.0 / math.sqrt(HSIZE)
 
@@ -80,33 +81,32 @@
     sum_class = view_class(own_view, sum_views[...])
     count, rows = sums.shape[0], sums.shape[1] // 2
     bias_part[...] = jnp.zeros_like(bias_part)
-    ride = heads * HSIZE
-    sum_grad[:, :, ride:] = jnp.zeros((count, 2 * rows, BLK), jnp.bfloat16)
     class_row = lax.broadcasted_iota(jnp.int32, (8, BLK), 0)
     class_lane = lax.broadcasted_iota(jnp.int32, (8, BLK), 1)
     for head in range(heads):
         cols = slice(head * HSIZE, (head + 1) * HSIZE)
+        late = slice((heads + head) * HSIZE, (heads + head + 1) * HSIZE)
         q = query[:, cols]
         go = grad_out[:, cols]
         keys = jnp.concatenate(
             [
-                left_kv[0, :, cols],
-                own_kv[0, :, cols],
-                right_kv[0, :, cols],
+                left_kv[:, cols],
+                own_kv[:, cols],
+                right_kv[:, cols],
                 sums[:, :rows, cols].reshape(count * rows, HSIZE),
             ],
             axis=0,
         )
         values = jnp.concatenate(
             [
-                left_kv[1, :, cols],
-                own_kv[1, :, cols],
-                right_kv[1, :, cols],
+                left_kv[:, late],
+                own_kv[:, late],
+                right_kv[:, late],
                 sums[:, rows:, cols].reshape(count * rows, HSIZE),
             ],
             axis=0,
         )
-        biases = [table[c, head_start + head] for c in range(NREL)]
+        biases = [table[head_start + head, c] for c in range(NREL)]
 
         def pick(cls):
             low = jnp.where(cls == 0, biases[0], biases[1])
@@ -134,11 +134,12 @@
         query_grad[:, cols] = (dot_tn(grad_low, keys) * SCALE).astype(jnp.bfloat16)
         key_terms = dot_nn(grad_low, q)
         value_terms = dot_nn(low, go)
-        for index, terms in enumerate((key_terms, value_terms)):
-            to_left[index, :, cols] = terms[:BLK].astype(jnp.bfloat16)
-            own_grad[index, :, cols] = terms[BLK : 2 * BLK]
-            to_right[index, :, cols] = terms[2 * BLK : 3 * BLK].astype(jnp.bfloat16)
-            sum_grad[:, index * rows : (index + 1) * rows, cols] = (
+        for index, (terms, where) in enumerate(((key_terms, cols), (value_terms, late))):
+            to_left[:, where] = terms[:BLK].astype(jnp.bfloat16)
+            own_grad[:, where] = terms[BLK : 2 * BLK]
+            to_right[:, where] = terms[2 * BLK : 3 * BLK].astype(jnp.bfloat16)
+            first = (index * heads + head) * rows
+            sum_grad[:, first : first + rows] = (
                 terms[3 * BLK :].astype(jnp.bfloat16).reshape(count, rows, HSIZE)
             )
         slot_sums = [
@@ -156,6 +157,21 @@
         line = jnp.sum(totals, axis=0, keepdims=True)
         for copy in range(ndp):
             bias_part[ndp * (head_start + head) + copy] = line
+
+
+def finish_kernel(heads, rows, terms, key_grad, value_grad, bias_grad):
+    def total(first, size):
+        parts = [terms[i, first : first + size].astype(jnp.float32) for i in range(terms.shape[0])]
+        while len(parts) > 1:
+            parts = [parts[i] + parts[i + 1] for i in range(0, len(parts), 2)]
+        return parts[0]
+
+    for head in range(heads):
+        cols = slice(head * HSIZE, (head + 1) * HSIZE)
+        key_grad[:, cols] = (total(head * rows, rows) * SCALE).astype(jnp.bfloat16)
+        value_grad[:, cols] = total((heads + head) * rows, rows).astype(jnp.bfloat16)
+    pieces = jnp.sum(total(2 * heads * rows, RIDE), axis=0, keepdims=True)
+    bias_grad[...] = pieces[:, :NREL]
 
 
 def body(
@@ -181,13 +197,14 @@
 
     up = [(i, i + 1) for i in range(nseq - 1)]
     down = [(i + 1, i) for i in range(nseq - 1)]
-    own_kv = jnp.stack([key_rows[0], value_rows[0]])
+    table_out = jnp.broadcast_to(rel_bias.reshape(1, NREL), (nfsdp, NREL))
+    table = lax.all_to_all(table_out, "fsdp", 0, 0, tiled=True)
+    own_kv = jnp.concatenate([key_rows[0], value_rows[0]], axis=1)
     left_kv = lax.ppermute(own_kv, "seq", up)
     right_kv = lax.ppermute(own_kv, "seq", down)
     own_sums = jnp.concatenate([summary_keys[0], summary_values[0]], axis=0)
     sums_out = jnp.broadcast_to(own_sums[None], (nseq, 2 * sum_rows, width))
     sums = lax.all_to_all(sums_out, "seq", 0, 0, tiled=True)
-    table = lax.all_gather(rel_bias, "fsdp", axis=1, tiled=True)
     place = jnp.stack([lax.axis_index("seq"), lax.axis_index("dp") * heads]).astype(jnp.int32)
 
     smem = pl.BlockSpec(memory_space=pltpu.SMEM)
@@ -198,10 +215,10 @@
         out_shape=(
             shaped((tok_rows, width), bf16),
             shaped((tok_rows, width), bf16),
-            shaped((2, BLK, width), bf16),
-            shaped((2, BLK, width), bf16),
-            shaped((2, BLK, width), f32),
-            shaped((nseq, 2 * sum_rows, width + BLK), bf16),
+            shaped((BLK, 2 * width), bf16),
+            shaped((BLK, 2 * width), bf16),
+            shaped((BLK, 2 * width), f32),
+            shaped((nseq, 2 * heads * sum_rows + RIDE, HSIZE), bf16),
             shaped((nfsdp * ndp, 1, BLK), f32),
         ),
         in_specs=[smem] * 4 + [vmem] * 7,
@@ -220,26 +237,33 @@
         right_kv,
         sums,
     )
+    bias_part = lax.all_to_all(bias_part, ("fsdp", "dp"), 0, 0, tiled=True)
     from_right = lax.ppermute(to_left, "seq", down)
     from_left = lax.ppermute(to_right, "seq", up)
-    bias_part = lax.all_to_all(bias_part, ("fsdp", "dp"), 0, 0, tiled=True)
     rest = jnp.sum(bias_part, axis=0)
     pieces = []
     for _ in range(3):
         pieces.append(lax.reduce_precision(rest, 8, 7))
         rest = rest - pieces[-1]
-    rider = jnp.pad(jnp.concatenate(pieces, axis=0).astype(bf16), ((0, 2 * sum_rows - 3), (0, 0)))
-    rider = jnp.broadcast_to(rider[None], (nseq, 2 * sum_rows, BLK))
-    sum_grad = lax.dynamic_update_slice(sum_grad, rider, (0, 0, width))
+    rider = jnp.pad(jnp.concatenate(pieces, axis=0).astype(bf16), ((0, RIDE - 3), (0, 0)))
+    rider = jnp.broadcast_to(rider[None], (nseq, RIDE, BLK))
+    sum_grad = lax.dynamic_update_slice(sum_grad, rider, (0, 2 * heads * sum_rows, 0))
     sum_terms = lax.all_to_all(sum_grad, "seq", 0, 0, tiled=True)
 
     grads = own_grad + from_left.astype(f32) + from_right.astype(f32)
-    key_grad = (grads[0] * SCALE).astype(bf16)
-    value_grad = grads[1].astype(bf16)
-    summary = jnp.sum(sum_terms.astype(f32), axis=0)
-    summary_key_grad = (summary[:sum_rows, :width] * SCALE).astype(bf16)
-    summary_value_grad = summary[sum_rows:, :width].astype(bf16)
-    bias_grad = jnp.sum(summary[:3, width : width + NREL], axis=0).reshape(NREL, 1)
+    key_grad = (grads[:, :width] * SCALE).astype(bf16)
+    value_grad = grads[:, width:].astype(bf16)
+    summary_key_grad, summary_value_grad, bias_grad = pl.pallas_call(
+        functools.partial(finish_kernel, heads, sum_rows),
+        out_shape=(
+            shaped((sum_rows, width), bf16),
+            shaped((sum_rows, width), bf16),
+            shaped((1, NREL), f32),
+        ),
+        in_specs=[vmem],
+        out_specs=(vmem,) * 3,
+        name="finish",
+    )(sum_terms)
     return (
         attended[None],
         query_grad[None],
@@ -247,7 +271,7 @@
         value_grad[None],
         summary_key_grad[None],
         summary_value_grad[None],
-        bias_grad,
+        bias_grad.reshape(NREL, 1),
     )
 
 

time: 107 us -> 108 us (level)
  the two profiles are of different devices: /device:TPU:4 before, /device:TPU:56 now
where the time goes in v1:
time: 108 us; the launch traced here: 107 us
  starting transfers between devices  46.2 us (43%)
  waiting for transfers between devices  40.2 us (37%)
  Pallas kernels  9.73 us (9%)
  local copies, waits for them, and re-layouts  8.2 us (8%)
  other arithmetic  2.37 us (2%)
    ppermute x1, waiting for transfers between devices, body(): from_right = lax.ppermute(to_left, 'seq', down)  15.6 us
    ppermute x1, waiting for transfers between devices, body(): right_kv = lax.ppermute(own_kv, 'seq', down)  13.2 us
    all_to_all x1, starting transfers between devices, body(): table = lax.all_to_all(table_out, 'fsdp', 0, 0, tiled=True)  10.4 us
    all_to_all x1, starting transfers between devices, body(): sums = lax.all_to_all(sums_out, 'seq', 0, 0, tiled=True)  9.48 us
    pallas_call x1, Pallas kernels, body(): pl.pallas_call(functools.partial(attention_kernel, heads, nblk, ndp), out...  8 us
    all_to_all x1, starting transfers between devices, body(): sum_terms = lax.all_to_all(sum_grad, 'seq', 0, 0, tiled=True)  6.88 us
    all_to_all x1, waiting for transfers between devices, body(): table = lax.all_to_all(table_out, 'fsdp', 0, 0, tiled=True)  6.79 us
    ppermute x1, starting transfers between devices, body(): left_kv = lax.ppermute(own_kv, 'seq', up)  6.09 us
  transfers between devices with their start and end apart: 8, of which 6 were waited for; matrix products, arithmetic and copies ran while one was open for 5% of the time, Pallas kernels for 0%

profile of v1, /device:TPU:56, one launch (start us, length us, event | category | flops | bytes accessed | tf_op | source)
XLA Modules:
  0.0 107.5 jit_solution(8640187905289028080)
XLA Ops:
  0.6 0.0 copy-start.12
  0.6 0.0 copy-start.9
  0.7 0.6 copy-done.12
  1.3 0.6 broadcast_in_dim.38
  1.9 10.4 %all-to-all-start = ((f32[16,1,4]{2,1,0:T(1,128)}), f32[16,1,4]{2,1,0:T(1,128)S(1)}, u32[]{:S(2)}, u32[]{:S(2)}) async-start(f32[16,1,4]{2,1,0:T(1,128)} %broadcast_in_dim.38), calls=%async_computation | async-start | bytes 16384 | tf_op jit(solution)/shard_map/all_to_all | solution.py:201
  12.3 0.0 copy-done.9
  12.3 0.7 pad_maximum_fusion.1
  13.1 6.8 %all-to-all-done = f32[16,1,4]{2,1,0:T(1,128)S(1)} async-done(((f32[16,1,4]{2,1,0:T(1,128)}), f32[16,1,4]{2,1,0:T(1,128)S(1)}, u32[]{:S(2)}, u32[]{:S(2)}) %all-to-all-start) | async-done | bytes 288 | tf_op jit(solution)/shard_map/all_to_all | solution.py:201
  19.8 0.0 copy-start.8
  19.9 0.9 broadcast_in_dim.39
  20.7 0.0 copy-done.8
  20.7 9.5 %all-to-all-start.1 = ((bf16[16,16,1024]{2,1,0:T(8,128)(2,1)}), bf16[16,16,1024]{2,1,0:T(8,128)(2,1)S(1)}, u32[]{:S(2)}, u32[]{:S(2)}) async-start(bf16[16,16,1024]{2,1,0:T(8,128)(2,1)} %broadcast_in_dim.39), calls=%async_computation.1 | async-start | bytes 1048576 | tf_op jit(solution)/shard_map/all_to_all | solution.py:207
  30.2 0.0 copy-done.6
  30.2 0.0 copy-done.7
  30.3 0.0 copy-start.2
  30.3 3.4 %collective-permute-start.1 = (bf16[128,2048]{1,0:T(8,128)(2,1)S(1)}, bf16[128,2048]{1,0:T(8,128)(2,1)S(1)}, u32[]{:S(2)}, u32[]{:S(2)}) collective-permute-start(bf16[128,2048]{1,0:T(8,128)(2,1)S(1)} %pad_maximum_fusion.own_kv), channel_id=1, source_target_pairs={{32,0},{64,32},{96,64},{128,96},{160,128},{192,160},{224,192},{256... | collective-permute-start | bytes 1572872 | tf_op jit(solution)/shard_map/ppermute | solution.py:204
  33.6 6.1 %collective-permute-start = (bf16[128,2048]{1,0:T(8,128)(2,1)S(1)}, bf16[128,2048]{1,0:T(8,128)(2,1)S(1)}, u32[]{:S(2)}, u32[]{:S(2)}) collective-permute-start(bf16[128,2048]{1,0:T(8,128)(2,1)S(1)} %pad_maximum_fusion.own_kv), channel_id=1, source_target_pairs={{0,32},{32,64},{64,96},{96,128},{128,160},{160,192},{192,224},{224... | collective-permute-start | bytes 1572872 | tf_op jit(solution)/shard_map/ppermute | solution.py:203
  39.7 0.0 copy-start.10
  39.8 0.7 copy-done.10
  40.4 0.7 copy.24
  41.1 0.7 copy-done.11
  41.8 0.7 copy.23.sum_views
  42.5 0.6 pad_add_fusion.place
  43.1 13.2 %collective-permute-done.1.right_kv = bf16[128,2048]{1,0:T(8,128)(2,1)S(1)} collective-permute-done((bf16[128,2048]{1,0:T(8,128)(2,1)S(1)}, bf16[128,2048]{1,0:T(8,128)(2,1)S(1)}, u32[]{:S(2)}, u32[]{:S(2)}) %collective-permute-start.1) | collective-permute-done | bytes 524320 | tf_op jit(solution)/shard_map/ppermute | solution.py:204
  56.3 0.0 collective-permute-done.left_kv
  56.3 0.0 all-to-all-done.1.sums
  56.3 0.0 copy-start.1
  56.4 0.0 copy-done.2
  56.4 0.8 copy-done.4
  57.1 0.2 copy-done.5
  57.3 0.2 copy-done.1
  57.5 8.0 %attention.1 = (bf16[128,1024]{1,0:T(8,128)(2,1)}, bf16[128,1024]{1,0:T(8,128)(2,1)}, bf16[128,2048]{1,0:T(8,128)(2,1)}, bf16[128,2048]{1,0:T(8,128)(2,1)}, f32[...) custom-call(s32[2]{0:T(128)} %pad_add_fusion.place, s32[16,3]{1,0:T(8,128)} %bitcast.34, ...), custom_call_target="tpu_custom_call" | custom-call | tf_op jit(solution)/shard_map/attention/pallas_call | solution.py:213
  65.5 4.0 %all-to-all-start.2 = ((f32[32,1,128]{2,1,0:T(1,128)}), f32[32,1,128]{2,1,0:T(1,128)S(1)}, u32[]{:S(2)}, u32[]{:S(2)}) async-start(f32[32,1,128]{2,1,0:T(1,128)} %get-tuple-element.23), calls=%async_computation.2 | async-start | bytes 32768 | tf_op jit(solution)/shard_map/all_to_all | solution.py:240
  69.5 4.1 %collective-permute-start.2 = (bf16[128,2048]{1,0:T(8,128)(2,1)}, bf16[128,2048]{1,0:T(8,128)(2,1)S(1)}, u32[]{:S(2)}, u32[]{:S(2)}) collective-permute-start(bf16[128,2048]{1,0:T(8,128)(2,1)} %get-tuple-element.20), channel_id=1, source_target_pairs={{0,32},{32,64},{64,96},{96,128},{128,160},{160,192},{192,224},{224... | collective-permute-start | bytes 1572872 | tf_op jit(solution)/shard_map/ppermute | solution.py:242
  73.5 1.9 %collective-permute-start.3 = (bf16[128,2048]{1,0:T(8,128)(2,1)}, bf16[128,2048]{1,0:T(8,128)(2,1)S(1)}, u32[]{:S(2)}, u32[]{:S(2)}) collective-permute-start(bf16[128,2048]{1,0:T(8,128)(2,1)} %get-tuple-element.21), channel_id=1, source_target_pairs={{32,0},{64,32},{96,64},{128,96},{160,128},{192,160},{224,192},{256... | collective-permute-start | bytes 1572872 | tf_op jit(solution)/shard_map/ppermute | solution.py:241
  75.5 2.3 %all-to-all-done.2 = f32[32,1,128]{2,1,0:T(1,128)S(1)} async-done(((f32[32,1,128]{2,1,0:T(1,128)}), f32[32,1,128]{2,1,0:T(1,128)S(1)}, u32[]{:S(2)}, u32[]{:S(2)}) %all-to-all-start.2) | async-done | bytes 16416 | tf_op jit(solution)/shard_map/all_to_all | solution.py:240
  77.7 0.1 reduce_sum.11
  77.8 0.6 broadcast_dynamic-update-slice_fusion
  78.4 6.9 %all-to-all-start.3 = ((bf16[16,136,128]{2,1,0:T(8,128)(2,1)}), bf16[16,136,128]{2,1,0:T(8,128)(2,1)S(1)}, u32[]{:S(2)}, u32[]{:S(2)}) async-start(bf16[16,136,128]{2,1,0:T(8,128)(2,1)} %broadcast_dynamic-update-slice_fusion), calls=%async_computation.3 | async-start | bytes 1114112 | tf_op jit(solution)/shard_map/all_to_all | solution.py:251
  85.3 0.3 collective-permute-done.2
  85.6 15.6 %collective-permute-done.3 = bf16[128,2048]{1,0:T(8,128)(2,1)S(1)} collective-permute-done((bf16[128,2048]{1,0:T(8,128)(2,1)}, bf16[128,2048]{1,0:T(8,128)(2,1)S(1)}, u32[]{:S(2)}, u32[]{:S(2)}) %collective-permute-start.3) | collective-permute-done | bytes 524320 | tf_op jit(solution)/shard_map/ppermute | solution.py:241
  101.2 0.0 copy-done.3
  101.2 0.2 convert_add_fusion
  101.3 0.7 fusion.2
  102.1 0.8 fusion.1
  102.8 2.1 %all-to-all-done.3.terms = bf16[16,136,128]{2,1,0:T(8,128)(2,1)S(1)} async-done(((bf16[16,136,128]{2,1,0:T(8,128)(2,1)}), bf16[16,136,128]{2,1,0:T(8,128)(2,1)S(1)}, u32[]{:S(2)}, u32[]{:S(2)}) %all-to-all-start.3) | async-done | bytes 557088 | tf_op jit(solution)/shard_map/all_to_all | solution.py:251
  104.9 0.8 copy-done
  105.7 1.7 %finish.1 = (bf16[8,1024]{1,0:T(8,128)(2,1)}, bf16[8,1024]{1,0:T(8,128)(2,1)}, f32[1,4]{1,0:T(1,128)}) custom-call(bf16[16,136,128]{2,1,0:T(8,128)(2,1)} %copy-done), custom_call_target="tpu_custom_call" | custom-call | tf_op jit(solution)/shard_map/finish/pallas_call | solution.py:256
  (10 shorter events, 0.1 us)
Async XLA Ops:
  0.6 0.7 copy-start.12
  0.6 11.7 %copy-start.9 = (bf16[1,8,1024]{2,1,0:T(8,128)(2,1)S(1)}, bf16[1,8,1024]{2,1,0:T(8,128)(2,1)}, u32[]{:S(2)}) copy-start(bf16[1,8,1024]{2,1,0:T(8,128)(2,1)} %param.14) | copy-start | bytes 49156
  1.9 18.0 %all-to-all-start = ((f32[16,1,4]{2,1,0:T(1,128)}), f32[16,1,4]{2,1,0:T(1,128)S(1)}, u32[]{:S(2)}, u32[]{:S(2)}) async-start(f32[16,1,4]{2,1,0:T(1,128)} %broadcast_in_dim.38), calls=%async_computation | async-start | bytes 16384 | tf_op jit(solution)/shard_map/all_to_all | solution.py:201
  19.8 0.9 copy-start.8
  20.7 9.5 %copy-start.6 = (bf16[1,128,1024]{2,1,0:T(8,128)(2,1)S(1)}, bf16[1,128,1024]{2,1,0:T(8,128)(2,1)}, u32[]{:S(2)}) copy-start(bf16[1,128,1024]{2,1,0:T(8,128)(2,1)} %param.12) | copy-start | bytes 786436
  20.7 9.5 %copy-start.7 = (bf16[1,128,1024]{2,1,0:T(8,128)(2,1)S(1)}, bf16[1,128,1024]{2,1,0:T(8,128)(2,1)}, u32[]{:S(2)}) copy-start(bf16[1,128,1024]{2,1,0:T(8,128)(2,1)} %param.11) | copy-start | bytes 786436
  20.7 35.6 %all-to-all-start.1 = ((bf16[16,16,1024]{2,1,0:T(8,128)(2,1)}), bf16[16,16,1024]{2,1,0:T(8,128)(2,1)S(1)}, u32[]{:S(2)}, u32[]{:S(2)}) async-start(bf16[16,16,1024]{2,1,0:T(8,128)(2,1)} %broadcast_in_dim.39), calls=%async_computation.1 | async-start | bytes 1048576 | tf_op jit(solution)/shard_map/all_to_all | solution.py:207
  30.3 26.1 %copy-start.2 = (bf16[128,2048]{1,0:T(8,128)(2,1)}, bf16[128,2048]{1,0:T(8,128)(2,1)S(1)}, u32[]{:S(2)}) copy-start(bf16[128,2048]{1,0:T(8,128)(2,1)S(1)} %pad_maximum_fusion.own_kv) | copy-start | bytes 1572868
  30.3 26.1 %collective-permute-start.1 = (bf16[128,2048]{1,0:T(8,128)(2,1)S(1)}, bf16[128,2048]{1,0:T(8,128)(2,1)S(1)}, u32[]{:S(2)}, u32[]{:S(2)}) collective-permute-start(bf16[128,2048]{1,0:T(8,128)(2,1)S(1)} %pad_maximum_fusion.own_kv), channel_id=1, source_target_pairs={{32,0},{64,32},{96,64},{128,96},{160,128},{192,160},{224,192},{256... | collective-permute-start | bytes 1572872 | tf_op jit(solution)/shard_map/ppermute | solution.py:204
  33.6 22.7 %collective-permute-start = (bf16[128,2048]{1,0:T(8,128)(2,1)S(1)}, bf16[128,2048]{1,0:T(8,128)(2,1)S(1)}, u32[]{:S(2)}, u32[]{:S(2)}) collective-permute-start(bf16[128,2048]{1,0:T(8,128)(2,1)S(1)} %pad_maximum_fusion.own_kv), channel_id=1, source_target_pairs={{0,32},{32,64},{64,96},{96,128},{128,160},{160,192},{192,224},{224... | collective-permute-start | bytes 1572872 | tf_op jit(solution)/shard_map/ppermute | solution.py:203
  39.7 0.7 copy-start.10
  41.1 0.7 copy-start.11
  56.3 0.8 copy-start.4
  56.3 1.0 copy-start.5
  56.3 1.2 %copy-start.1 = (bf16[16,16,1024]{2,1,0:T(8,128)(2,1)}, bf16[16,16,1024]{2,1,0:T(8,128)(2,1)S(1)}, u32[]{:S(2)}) copy-start(bf16[16,16,1024]{2,1,0:T(8,128)(2,1)S(1)} %all-to-all-done.1.sums) | copy-start | bytes 1572868
  65.5 35.7 %copy-start.3 = (f32[128,2048]{1,0:T(8,128)S(1)}, f32[128,2048]{1,0:T(8,128)}, u32[]{:S(2)}) copy-start(f32[128,2048]{1,0:T(8,128)} %get-tuple-element.19) | copy-start | bytes 3145732
  65.5 12.2 %all-to-all-start.2 = ((f32[32,1,128]{2,1,0:T(1,128)}), f32[32,1,128]{2,1,0:T(1,128)S(1)}, u32[]{:S(2)}, u32[]{:S(2)}) async-start(f32[32,1,128]{2,1,0:T(1,128)} %get-tuple-element.23), calls=%async_computation.2 | async-start | bytes 32768 | tf_op jit(solution)/shard_map/all_to_all | solution.py:240
  69.5 16.1 %collective-permute-start.2 = (bf16[128,2048]{1,0:T(8,128)(2,1)}, bf16[128,2048]{1,0:T(8,128)(2,1)S(1)}, u32[]{:S(2)}, u32[]{:S(2)}) collective-permute-start(bf16[128,2048]{1,0:T(8,128)(2,1)} %get-tuple-element.20), channel_id=1, source_target_pairs={{0,32},{32,64},{64,96},{96,128},{128,160},{160,192},{192,224},{224... | collective-permute-start | bytes 1572872 | tf_op jit(solution)/shard_map/ppermute | solution.py:242
  73.5 27.6 %collective-permute-start.3 = (bf16[128,2048]{1,0:T(8,128)(2,1)}, bf16[128,2048]{1,0:T(8,128)(2,1)S(1)}, u32[]{:S(2)}, u32[]{:S(2)}) collective-permute-start(bf16[128,2048]{1,0:T(8,128)(2,1)} %get-tuple-element.21), channel_id=1, source_target_pairs={{32,0},{64,32},{96,64},{128,96},{160,128},{192,160},{224,192},{256... | collective-permute-start | bytes 1572872 | tf_op jit(solution)/shard_map/ppermute | solution.py:241
  78.4 26.5 %all-to-all-start.3 = ((bf16[16,136,128]{2,1,0:T(8,128)(2,1)}), bf16[16,136,128]{2,1,0:T(8,128)(2,1)S(1)}, u32[]{:S(2)}, u32[]{:S(2)}) async-start(bf16[16,136,128]{2,1,0:T(8,128)(2,1)} %broadcast_dynamic-update-slice_fusion), calls=%async_computation.3 | async-start | bytes 1114112 | tf_op jit(solution)/shard_map/all_to_all | solution.py:251
  104.9 0.8 copy-start

commit v2 on v1

--- a/solution.py
+++ b/solution.py
@@ -46,6 +46,7 @@
     heads,
     nblk,
     ndp,
+    half,
     place,
     pattern,
     views,
@@ -56,11 +57,14 @@
     own_kv,
     left_kv,
     right_kv,
+    cross_key,
+    cross_value,
     sums,
     attended,
     query_grad,
     to_left,
     to_right,
+    to_cross,
     own_grad,
     sum_grad,
     bias_part,
@@ -90,18 +94,18 @@
         go = grad_out[:, cols]
         keys = jnp.concatenate(
             [
-                left_kv[:, cols],
+                lax.select(block == half, cross_key[:, cols], left_kv[:, cols]),
                 own_kv[:, cols],
-                right_kv[:, cols],
+                lax.select(block == half - 1, cross_key[:, cols], right_kv[:, cols]),
                 sums[:, :rows, cols].reshape(count * rows, HSIZE),
             ],
             axis=0,
         )
         values = jnp.concatenate(
             [
-                left_kv[:, late],
+                lax.select(block == half, cross_value[:, cols], left_kv[:, late]),
                 own_kv[:, late],
-                right_kv[:, late],
+                lax.select(block == half - 1, cross_value[:, cols], right_kv[:, late]),
                 sums[:, rows:, cols].reshape(count * rows, HSIZE),
             ],
             axis=0,
@@ -135,9 +139,12 @@
         key_terms = dot_nn(grad_low, q)
         value_terms = dot_nn(low, go)
         for index, (terms, where) in enumerate(((key_terms, cols), (value_terms, late))):
-            to_left[:, where] = terms[:BLK].astype(jnp.bfloat16)
+            leftward = terms[:BLK].astype(jnp.bfloat16)
+            rightward = terms[2 * BLK : 3 * BLK].astype(jnp.bfloat16)
+            to_left[:, where] = leftward
+            to_right[:, where] = rightward
+            to_cross[index, :, cols] = lax.select(block == half, leftward, rightward)
             own_grad[:, where] = terms[BLK : 2 * BLK]
-            to_right[:, where] = terms[2 * BLK : 3 * BLK].astype(jnp.bfloat16)
             first = (index * heads + head) * rows
             sum_grad[:, first : first + rows] = (
                 terms[3 * BLK :].astype(jnp.bfloat16).reshape(count, rows, HSIZE)
@@ -195,13 +202,33 @@
     sum_rows = summary_keys.shape[1]
     bf16, f32 = jnp.bfloat16, jnp.float32
 
-    up = [(i, i + 1) for i in range(nseq - 1)]
-    down = [(i + 1, i) for i in range(nseq - 1)]
+    half = nseq // 2
+    up = [(i, i + 1) for i in range(nseq - 1) if i + 1 != half]
+    down = [(i + 1, i) for i in range(nseq - 1) if i + 1 != half]
+    both = ("seq", "dp")
+
+    def spot(row, side, col):
+        return (side * half + row) * ndp + col
+
+    last = half - 1
+    across = [(spot(last, 0, c), spot(0, 1, c)) for c in range(ndp)]
+    across += [(b, a) for a, b in across]
+    first_leg, second_leg = [], []
+    for side in range(2):
+        start, stop = (last, 0) if side == 0 else (0, last)
+        for col in range(ndp):
+            via = spot(start, side if col else 1 - side, (col - 1) % ndp)
+            first_leg.append((spot(start, side, col), via))
+            second_leg.append((via, spot(stop, 1 - side, col)))
+
     table_out = jnp.broadcast_to(rel_bias.reshape(1, NREL), (nfsdp, NREL))
     table = lax.all_to_all(table_out, "fsdp", 0, 0, tiled=True)
+    passing = lax.ppermute(value_rows[0], both, first_leg)
+    cross_key = lax.ppermute(key_rows[0], both, across)
     own_kv = jnp.concatenate([key_rows[0], value_rows[0]], axis=1)
     left_kv = lax.ppermute(own_kv, "seq", up)
     right_kv = lax.ppermute(own_kv, "seq", down)
+    cross_value = lax.ppermute(passing, both, second_leg)
     own_sums = jnp.concatenate([summary_keys[0], summary_values[0]], axis=0)
     sums_out = jnp.broadcast_to(own_sums[None], (nseq, 2 * sum_rows, width))
     sums = lax.all_to_all(sums_out, "seq", 0, 0, tiled=True)
@@ -210,19 +237,20 @@
     smem = pl.BlockSpec(memory_space=pltpu.SMEM)
     vmem = pl.BlockSpec(memory_space=pltpu.VMEM)
     shaped = jax.ShapeDtypeStruct
-    attended, query_grad, to_left, to_right, own_grad, sum_grad, bias_part = pl.pallas_call(
-        functools.partial(attention_kernel, heads, nblk, ndp),
+    attended, query_grad, to_left, to_right, to_cross, own_grad, sum_grad, bias_part = pl.pallas_call(
+        functools.partial(attention_kernel, heads, nblk, ndp, half),
         out_shape=(
             shaped((tok_rows, width), bf16),
             shaped((tok_rows, width), bf16),
             shaped((BLK, 2 * width), bf16),
             shaped((BLK, 2 * width), bf16),
+            shaped((2, BLK, width), bf16),
             shaped((BLK, 2 * width), f32),
             shaped((nseq, 2 * heads * sum_rows + RIDE, HSIZE), bf16),
             shaped((nfsdp * ndp, 1, BLK), f32),
         ),
-        in_specs=[smem] * 4 + [vmem] * 7,
-        out_specs=(vmem,) * 7,
+        in_specs=[smem] * 4 + [vmem] * 9,
+        out_specs=(vmem,) * 8,
         name="attention",
     )(
         place,
@@ -235,11 +263,16 @@
         own_kv,
         left_kv,
         right_kv,
+        cross_key,
+        cross_value,
         sums,
     )
     bias_part = lax.all_to_all(bias_part, ("fsdp", "dp"), 0, 0, tiled=True)
+    passing = lax.ppermute(to_cross[1], both, first_leg)
+    from_cross_key = lax.ppermute(to_cross[0], both, across)
     from_right = lax.ppermute(to_left, "seq", down)
     from_left = lax.ppermute(to_right, "seq", up)
+    from_cross_value = lax.ppermute(passing, both, second_leg)
     rest = jnp.sum(bias_part, axis=0)
     pieces = []
     for _ in range(3):
@@ -251,8 +284,8 @@
     sum_terms = lax.all_to_all(sum_grad, "seq", 0, 0, tiled=True)
 
     grads = own_grad + from_left.astype(f32) + from_right.astype(f32)
-    key_grad = (grads[:, :width] * SCALE).astype(bf16)
-    value_grad = grads[:, width:].astype(bf16)
+    key_grad = ((grads[:, :width] + from_cross_key.astype(f32)) * SCALE).astype(bf16)
+    value_grad = (grads[:, width:] + from_cross_value.astype(f32)).astype(bf16)
     summary_key_grad, summary_value_grad, bias_grad = pl.pallas_call(
         functools.partial(finish_kernel, heads, sum_rows),
         out_shape=(

time: 108 us -> 118 us (1.093)
  the two profiles are of different devices: /device:TPU:56 before, /device:TPU:6 now
where the time goes in v2:
time: 118 us; the launch traced here: 117 us
  starting transfers between devices  55.5 us (47%)
  waiting for transfers between devices  39.1 us (33%)
  Pallas kernels  10.1 us (9%)
  local copies, waits for them, and re-layouts  8.61 us (7%)
  other arithmetic  2.55 us (2%)
    ppermute x1, waiting for transfers between devices, body(): from_cross_key = lax.ppermute(to_cross[0], both, across)  15.3 us
    all_to_all x1, starting transfers between devices, body(): table = lax.all_to_all(table_out, 'fsdp', 0, 0, tiled=True)  10.4 us
    all_to_all x1, starting transfers between devices, body(): sums = lax.all_to_all(sums_out, 'seq', 0, 0, tiled=True)  10.2 us
    all_to_all x1, starting transfers between devices, body(): sum_terms = lax.all_to_all(sum_grad, 'seq', 0, 0, tiled=True)  8.92 us
    pallas_call x1, Pallas kernels, body(): pl.pallas_call(functools.partial(attention_kernel, heads, nblk, ndp, half...  8.37 us
    all_to_all x1, waiting for transfers between devices, body(): table = lax.all_to_all(table_out, 'fsdp', 0, 0, tiled=True)  6.79 us
    ppermute x1, waiting for transfers between devices, body(): cross_key = lax.ppermute(key_rows[0], both, across)  5.48 us
    ppermute x1, starting transfers between devices, body(): left_kv = lax.ppermute(own_kv, 'seq', up)  4.58 us
  transfers between devices with their start and end apart: 14, of which 8 were waited for; matrix products, arithmetic and copies ran while one was open for 5% of the time, Pallas kernels for 0%

profile of v2, /device:TPU:6, one launch (start us, length us, event | category | flops | bytes accessed | tf_op | source)
XLA Modules:
  0.0 116.8 jit_solution(807211254423637489)
XLA Ops:
  0.7 0.6 copy-done.14
  1.3 0.6 broadcast_in_dim.38
  1.9 10.4 %all-to-all-start = ((f32[16,1,4]{2,1,0:T(1,128)}), f32[16,1,4]{2,1,0:T(1,128)S(1)}, u32[]{:S(2)}, u32[]{:S(2)}) async-start(f32[16,1,4]{2,1,0:T(1,128)} %broadcast_in_dim.38), calls=%async_computation | async-start | bytes 16384 | tf_op jit(solution)/shard_map/all_to_all | solution.py:225
  12.3 0.7 pad_maximum_fusion.1
  13.1 6.8 %all-to-all-done = f32[16,1,4]{2,1,0:T(1,128)S(1)} async-done(((f32[16,1,4]{2,1,0:T(1,128)}), f32[16,1,4]{2,1,0:T(1,128)S(1)}, u32[]{:S(2)}, u32[]{:S(2)}) %all-to-all-start) | async-done | bytes 288 | tf_op jit(solution)/shard_map/all_to_all | solution.py:225
  19.9 0.8 broadcast_in_dim.39
  20.7 10.2 %all-to-all-start.1 = ((bf16[16,16,1024]{2,1,0:T(8,128)(2,1)}), bf16[16,16,1024]{2,1,0:T(8,128)(2,1)S(1)}, u32[]{:S(2)}, u32[]{:S(2)}) async-start(bf16[16,16,1024]{2,1,0:T(8,128)(2,1)} %broadcast_in_dim.39), calls=%async_computation.1 | async-start | bytes 1048576 | tf_op jit(solution)/shard_map/all_to_all | solution.py:234
  30.9 2.7 %collective-permute-start.3 = (bf16[128,1024]{1,0:T(8,128)(2,1)S(1)}, bf16[128,1024]{1,0:T(8,128)(2,1)S(1)}, u32[]{:S(2)}, u32[]{:S(2)}) collective-permute-start(bf16[128,1024]{1,0:T(8,128)(2,1)S(1)} %bitcast.35), channel_id=1, source_target_pairs={{224,481},{225,224},{256,1},{257,256},{226,483},{227,226},{258,3},... | collective-permute-start | bytes 786440 | tf_op jit(solution)/shard_map/ppermute | solution.py:226
  33.7 1.3 %collective-permute-start.1 = (bf16[128,2048]{1,0:T(8,128)(2,1)S(1)}, bf16[128,2048]{1,0:T(8,128)(2,1)S(1)}, u32[]{:S(2)}, u32[]{:S(2)}) collective-permute-start(bf16[128,2048]{1,0:T(8,128)(2,1)S(1)} %pad_maximum_fusion.own_kv), channel_id=1, source_target_pairs={{32,0},{64,32},{96,64},{128,96},{160,128},{192,160},{224,192},{288... | collective-permute-start | bytes 1572872 | tf_op jit(solution)/shard_map/ppermute | solution.py:230
  35.0 4.6 %collective-permute-start = (bf16[128,2048]{1,0:T(8,128)(2,1)S(1)}, bf16[128,2048]{1,0:T(8,128)(2,1)S(1)}, u32[]{:S(2)}, u32[]{:S(2)}) collective-permute-start(bf16[128,2048]{1,0:T(8,128)(2,1)S(1)} %pad_maximum_fusion.own_kv), channel_id=1, source_target_pairs={{0,32},{32,64},{64,96},{96,128},{128,160},{160,192},{192,224},{256... | collective-permute-start | bytes 1572872 | tf_op jit(solution)/shard_map/ppermute | solution.py:229
  39.6 1.9 %collective-permute-start.2 = (bf16[128,1024]{1,0:T(8,128)(2,1)S(1)}, bf16[128,1024]{1,0:T(8,128)(2,1)S(1)}, u32[]{:S(2)}, u32[]{:S(2)}) collective-permute-start(bf16[128,1024]{1,0:T(8,128)(2,1)S(1)} %bitcast.38), channel_id=1, source_target_pairs={{224,256},{225,257},{256,224},{257,225},{226,258},{227,259},{258,2... | collective-permute-start | bytes 786440 | tf_op jit(solution)/shard_map/ppermute | solution.py:227
  41.6 1.4 %collective-permute-done.3 = bf16[128,1024]{1,0:T(8,128)(2,1)S(1)} collective-permute-done((bf16[128,1024]{1,0:T(8,128)(2,1)S(1)}, bf16[128,1024]{1,0:T(8,128)(2,1)S(1)}, u32[]{:S(2)}, u32[]{:S(2)}) %collective-permute-start.3) | collective-permute-done | bytes 262176 | tf_op jit(solution)/shard_map/ppermute | solution.py:226
  42.9 1.3 %collective-permute-start.4 = (bf16[128,1024]{1,0:T(8,128)(2,1)S(1)}, bf16[128,1024]{1,0:T(8,128)(2,1)S(1)}, u32[]{:S(2)}, u32[]{:S(2)}) collective-permute-start(bf16[128,1024]{1,0:T(8,128)(2,1)S(1)} %collective-permute-done.3), channel_id=1, source_target_pairs={{481,256},{224,257},{1,224},{256,225},{483,258},{226,259},{3,226},... | collective-permute-start | bytes 786440 | tf_op jit(solution)/shard_map/ppermute | solution.py:231
  44.2 0.0 copy-start.12
  44.2 0.7 copy-done.12
  44.9 0.7 copy.24
  45.6 0.7 copy-done.13
  46.2 0.7 copy.23.sum_views
  47.0 0.6 pad_add_fusion.place
  47.6 5.5 %collective-permute-done.2.cross_key = bf16[128,1024]{1,0:T(8,128)(2,1)S(1)} collective-permute-done((bf16[128,1024]{1,0:T(8,128)(2,1)S(1)}, bf16[128,1024]{1,0:T(8,128)(2,1)S(1)}, u32[]{:S(2)}, u32[]{:S(2)}) %collective-permute-start.2) | collective-permute-done | bytes 262176 | tf_op jit(solution)/shard_map/ppermute | solution.py:227
  53.1 4.5 %collective-permute-done.4.cross_value = bf16[128,1024]{1,0:T(8,128)(2,1)S(1)} collective-permute-done((bf16[128,1024]{1,0:T(8,128)(2,1)S(1)}, bf16[128,1024]{1,0:T(8,128)(2,1)S(1)}, u32[]{:S(2)}, u32[]{:S(2)}) %collective-permute-start.4) | collective-permute-done | bytes 262176 | tf_op jit(solution)/shard_map/ppermute | solution.py:231
  57.6 0.0 collective-permute-done.1.right_kv
  57.6 0.0 collective-permute-done.left_kv
  57.6 0.6 copy-done.7
  58.3 0.2 copy-done.4
  58.5 0.2 copy-done.5
  58.6 0.2 copy-done.1
  58.8 8.4 %attention.1 = (bf16[128,1024]{1,0:T(8,128)(2,1)}, bf16[128,1024]{1,0:T(8,128)(2,1)}, bf16[128,2048]{1,0:T(8,128)(2,1)}, bf16[128,2048]{1,0:T(8,128)(2,1)}, bf16...) custom-call(s32[2]{0:T(128)} %pad_add_fusion.place, ...), custom_call_target="tpu_custom_call" | custom-call | tf_op jit(solution)/shard_map/attention/pallas_call | solution.py:240
  67.2 3.6 %all-to-all-start.2 = ((f32[32,1,128]{2,1,0:T(1,128)}), f32[32,1,128]{2,1,0:T(1,128)S(1)}, u32[]{:S(2)}, u32[]{:S(2)}) async-start(f32[32,1,128]{2,1,0:T(1,128)} %get-tuple-element.25), calls=%async_computation.2 | async-start | bytes 32768 | tf_op jit(solution)/shard_map/all_to_all | solution.py:270
  70.8 1.2 slice_bitcast_fusion
  72.0 2.0 %collective-permute-start.8 = (bf16[128,1024]{1,0:T(8,128)(2,1)S(1)}, bf16[128,1024]{1,0:T(8,128)(2,1)S(1)}, u32[]{:S(2)}, u32[]{:S(2)}) collective-permute-start(bf16[128,1024]{1,0:T(8,128)(2,1)S(1)} %get-tuple-element.31), channel_id=1, source_target_pairs={{224,481},{225,224},{256,1},{257,256},{226,483},{227,226},{258,3},... | collective-permute-start | bytes 786440 | tf_op jit(solution)/shard_map/ppermute | solution.py:271
  74.0 1.3 %collective-permute-start.5 = (bf16[128,2048]{1,0:T(8,128)(2,1)}, bf16[128,2048]{1,0:T(8,128)(2,1)S(1)}, u32[]{:S(2)}, u32[]{:S(2)}) collective-permute-start(bf16[128,2048]{1,0:T(8,128)(2,1)} %get-tuple-element.21), channel_id=1, source_target_pairs={{0,32},{32,64},{64,96},{96,128},{128,160},{160,192},{192,224},{256... | collective-permute-start | bytes 1572872 | tf_op jit(solution)/shard_map/ppermute | solution.py:274
  75.3 1.3 %collective-permute-start.6 = (bf16[128,2048]{1,0:T(8,128)(2,1)}, bf16[128,2048]{1,0:T(8,128)(2,1)S(1)}, u32[]{:S(2)}, u32[]{:S(2)}) collective-permute-start(bf16[128,2048]{1,0:T(8,128)(2,1)} %get-tuple-element.22), channel_id=1, source_target_pairs={{32,0},{64,32},{96,64},{128,96},{160,128},{192,160},{224,192},{288... | collective-permute-start | bytes 1572872 | tf_op jit(solution)/shard_map/ppermute | solution.py:273
  76.6 1.2 all-to-all-done.2
  77.8 0.1 reduce_sum.11
  77.9 0.6 broadcast_dynamic-update-slice_fusion
  78.5 8.9 %all-to-all-start.3 = ((bf16[16,136,128]{2,1,0:T(8,128)(2,1)}), bf16[16,136,128]{2,1,0:T(8,128)(2,1)S(1)}, u32[]{:S(2)}, u32[]{:S(2)}) async-start(bf16[16,136,128]{2,1,0:T(8,128)(2,1)} %broadcast_dynamic-update-slice_fusion), calls=%async_computation.3 | async-start | bytes 1114112 | tf_op jit(solution)/shard_map/all_to_all | solution.py:284
  87.4 4.6 %collective-permute-start.7 = (bf16[128,1024]{1,0:T(8,128)(2,1)S(1)}, bf16[128,1024]{1,0:T(8,128)(2,1)S(1)}, u32[]{:S(2)}, u32[]{:S(2)}) collective-permute-start(bf16[128,1024]{1,0:T(8,128)(2,1)S(1)} %get-tuple-element.32), channel_id=1, source_target_pairs={{224,256},{225,257},{256,224},{257,225},{226,258},{227,259},{258,2... | collective-permute-start | bytes 786440 | tf_op jit(solution)/shard_map/ppermute | solution.py:272
  92.0 1.3 %collective-permute-start.9 = (bf16[128,1024]{1,0:T(8,128)(2,1)S(1)}, bf16[128,1024]{1,0:T(8,128)(2,1)S(1)}, u32[]{:S(2)}, u32[]{:S(2)}) collective-permute-start(bf16[128,1024]{1,0:T(8,128)(2,1)S(1)} %collective-permute-done.8), channel_id=1, source_target_pairs={{481,256},{224,257},{1,224},{256,225},{483,258},{226,259},{3,226},... | collective-permute-start | bytes 786440 | tf_op jit(solution)/shard_map/ppermute | solution.py:275
  93.3 0.0 collective-permute-done.5
  93.3 0.1 collective-permute-done.6
  93.4 0.2 convert_add_fusion
  93.6 15.3 %collective-permute-done.7 = bf16[128,1024]{1,0:T(8,128)(2,1)S(1)} collective-permute-done((bf16[128,1024]{1,0:T(8,128)(2,1)S(1)}, bf16[128,1024]{1,0:T(8,128)(2,1)S(1)}, u32[]{:S(2)}, u32[]{:S(2)}) %collective-permute-start.7) | collective-permute-done | bytes 262176 | tf_op jit(solution)/shard_map/ppermute | solution.py:272
  108.9 4.4 %collective-permute-done.9 = bf16[128,1024]{1,0:T(8,128)(2,1)S(1)} collective-permute-done((bf16[128,1024]{1,0:T(8,128)(2,1)S(1)}, bf16[128,1024]{1,0:T(8,128)(2,1)S(1)}, u32[]{:S(2)}, u32[]{:S(2)}) %collective-permute-start.9) | collective-permute-done | bytes 262176 | tf_op jit(solution)/shard_map/ppermute | solution.py:275
  113.3 0.9 fusion.4
  114.3 0.0 all-to-all-done.3.terms
  114.3 0.8 copy-done
  115.1 1.7 %finish.1 = (bf16[8,1024]{1,0:T(8,128)(2,1)}, bf16[8,1024]{1,0:T(8,128)(2,1)}, f32[1,4]{1,0:T(1,128)}) custom-call(bf16[16,136,128]{2,1,0:T(8,128)(2,1)} %copy-done), custom_call_target="tpu_custom_call" | custom-call | tf_op jit(solution)/shard_map/finish/pallas_call | solution.py:289
  (26 shorter events, 0.1 us)
Async XLA Ops:
  0.6 0.7 copy-start.14
  0.6 11.7 %copy-start.11 = (bf16[1,8,1024]{2,1,0:T(8,128)(2,1)S(1)}, bf16[1,8,1024]{2,1,0:T(8,128)(2,1)}, u32[]{:S(2)}) copy-start(bf16[1,8,1024]{2,1,0:T(8,128)(2,1)} %param.14) | copy-start | bytes 49156
  1.9 18.0 %all-to-all-start = ((f32[16,1,4]{2,1,0:T(1,128)}), f32[16,1,4]{2,1,0:T(1,128)S(1)}, u32[]{:S(2)}, u32[]{:S(2)}) async-start(f32[16,1,4]{2,1,0:T(1,128)} %broadcast_in_dim.38), calls=%async_computation | async-start | bytes 16384 | tf_op jit(solution)/shard_map/all_to_all | solution.py:225
  19.8 0.8 copy-start.10
  20.7 10.2 %copy-start.8 = (bf16[1,128,1024]{2,1,0:T(8,128)(2,1)S(1)}, bf16[1,128,1024]{2,1,0:T(8,128)(2,1)}, u32[]{:S(2)}) copy-start(bf16[1,128,1024]{2,1,0:T(8,128)(2,1)} %param.12) | copy-start | bytes 786436
  20.7 13.0 %copy-start.9 = (bf16[1,128,1024]{2,1,0:T(8,128)(2,1)S(1)}, bf16[1,128,1024]{2,1,0:T(8,128)(2,1)}, u32[]{:S(2)}) copy-start(bf16[1,128,1024]{2,1,0:T(8,128)(2,1)} %param.11) | copy-start | bytes 786436
  20.7 36.9 %all-to-all-start.1 = ((bf16[16,16,1024]{2,1,0:T(8,128)(2,1)}), bf16[16,16,1024]{2,1,0:T(8,128)(2,1)S(1)}, u32[]{:S(2)}, u32[]{:S(2)}) async-start(bf16[16,16,1024]{2,1,0:T(8,128)(2,1)} %broadcast_in_dim.39), calls=%async_computation.1 | async-start | bytes 1048576 | tf_op jit(solution)/shard_map/all_to_all | solution.py:234
  30.9 12.0 %collective-permute-start.3 = (bf16[128,1024]{1,0:T(8,128)(2,1)S(1)}, bf16[128,1024]{1,0:T(8,128)(2,1)S(1)}, u32[]{:S(2)}, u32[]{:S(2)}) collective-permute-start(bf16[128,1024]{1,0:T(8,128)(2,1)S(1)} %bitcast.35), channel_id=1, source_target_pairs={{224,481},{225,224},{256,1},{257,256},{226,483},{227,226},{258,3},... | collective-permute-start | bytes 786440 | tf_op jit(solution)/shard_map/ppermute | solution.py:226
  33.7 23.9 %copy-start.2 = (bf16[128,2048]{1,0:T(8,128)(2,1)}, bf16[128,2048]{1,0:T(8,128)(2,1)S(1)}, u32[]{:S(2)}) copy-start(bf16[128,2048]{1,0:T(8,128)(2,1)S(1)} %pad_maximum_fusion.own_kv) | copy-start | bytes 1572868
  33.7 23.8 %collective-permute-start.1 = (bf16[128,2048]{1,0:T(8,128)(2,1)S(1)}, bf16[128,2048]{1,0:T(8,128)(2,1)S(1)}, u32[]{:S(2)}, u32[]{:S(2)}) collective-permute-start(bf16[128,2048]{1,0:T(8,128)(2,1)S(1)} %pad_maximum_fusion.own_kv), channel_id=1, source_target_pairs={{32,0},{64,32},{96,64},{128,96},{160,128},{192,160},{224,192},{288... | collective-permute-start | bytes 1572872 | tf_op jit(solution)/shard_map/ppermute | solution.py:230
  35.0 22.5 %collective-permute-start = (bf16[128,2048]{1,0:T(8,128)(2,1)S(1)}, bf16[128,2048]{1,0:T(8,128)(2,1)S(1)}, u32[]{:S(2)}, u32[]{:S(2)}) collective-permute-start(bf16[128,2048]{1,0:T(8,128)(2,1)S(1)} %pad_maximum_fusion.own_kv), channel_id=1, source_target_pairs={{0,32},{32,64},{64,96},{96,128},{128,160},{160,192},{192,224},{256... | collective-permute-start | bytes 1572872 | tf_op jit(solution)/shard_map/ppermute | solution.py:229
  39.6 13.4 %collective-permute-start.2 = (bf16[128,1024]{1,0:T(8,128)(2,1)S(1)}, bf16[128,1024]{1,0:T(8,128)(2,1)S(1)}, u32[]{:S(2)}, u32[]{:S(2)}) collective-permute-start(bf16[128,1024]{1,0:T(8,128)(2,1)S(1)} %bitcast.38), channel_id=1, source_target_pairs={{224,256},{225,257},{256,224},{257,225},{226,258},{227,259},{258,2... | collective-permute-start | bytes 786440 | tf_op jit(solution)/shard_map/ppermute | solution.py:227
  42.9 14.7 %collective-permute-start.4 = (bf16[128,1024]{1,0:T(8,128)(2,1)S(1)}, bf16[128,1024]{1,0:T(8,128)(2,1)S(1)}, u32[]{:S(2)}, u32[]{:S(2)}) collective-permute-start(bf16[128,1024]{1,0:T(8,128)(2,1)S(1)} %collective-permute-done.3), channel_id=1, source_target_pairs={{481,256},{224,257},{1,224},{256,225},{483,258},{226,259},{3,226},... | collective-permute-start | bytes 786440 | tf_op jit(solution)/shard_map/ppermute | solution.py:231
  44.2 0.7 copy-start.12
  45.6 0.7 copy-start.13
  53.1 4.6 %copy-start.6 = (bf16[128,1024]{1,0:T(8,128)(2,1)}, bf16[128,1024]{1,0:T(8,128)(2,1)S(1)}, u32[]{:S(2)}) copy-start(bf16[128,1024]{1,0:T(8,128)(2,1)S(1)} %collective-permute-done.2.cross_key) | copy-start | bytes 786436
  57.6 0.7 copy-start.7
  57.6 0.9 copy-start.4
  57.6 1.0 copy-start.5
  57.6 1.2 %copy-start.1 = (bf16[16,16,1024]{2,1,0:T(8,128)(2,1)}, bf16[16,16,1024]{2,1,0:T(8,128)(2,1)S(1)}, u32[]{:S(2)}) copy-start(bf16[16,16,1024]{2,1,0:T(8,128)(2,1)S(1)} %all-to-all-done.1.sums) | copy-start | bytes 1572868
  67.2 10.6 %all-to-all-start.2 = ((f32[32,1,128]{2,1,0:T(1,128)}), f32[32,1,128]{2,1,0:T(1,128)S(1)}, u32[]{:S(2)}, u32[]{:S(2)}) async-start(f32[32,1,128]{2,1,0:T(1,128)} %get-tuple-element.25), calls=%async_computation.2 | async-start | bytes 32768 | tf_op jit(solution)/shard_map/all_to_all | solution.py:270
  70.8 22.6 %copy-start.3 = (f32[128,2048]{1,0:T(8,128)S(1)}, f32[128,2048]{1,0:T(8,128)}, u32[]{:S(2)}) copy-start(f32[128,2048]{1,0:T(8,128)} %get-tuple-element.20) | copy-start | bytes 3145732
  72.0 20.0 %collective-permute-start.8 = (bf16[128,1024]{1,0:T(8,128)(2,1)S(1)}, bf16[128,1024]{1,0:T(8,128)(2,1)S(1)}, u32[]{:S(2)}, u32[]{:S(2)}) collective-permute-start(bf16[128,1024]{1,0:T(8,128)(2,1)S(1)} %get-tuple-element.31), channel_id=1, source_target_pairs={{224,481},{225,224},{256,1},{257,256},{226,483},{227,226},{258,3},... | collective-permute-start | bytes 786440 | tf_op jit(solution)/shard_map/ppermute | solution.py:271
  74.0 19.3 %collective-permute-start.5 = (bf16[128,2048]{1,0:T(8,128)(2,1)}, bf16[128,2048]{1,0:T(8,128)(2,1)S(1)}, u32[]{:S(2)}, u32[]{:S(2)}) collective-permute-start(bf16[128,2048]{1,0:T(8,128)(2,1)} %get-tuple-element.21), channel_id=1, source_target_pairs={{0,32},{32,64},{64,96},{96,128},{128,160},{160,192},{192,224},{256... | collective-permute-start | bytes 1572872 | tf_op jit(solution)/shard_map/ppermute | solution.py:274
  75.3 18.1 %collective-permute-start.6 = (bf16[128,2048]{1,0:T(8,128)(2,1)}, bf16[128,2048]{1,0:T(8,128)(2,1)S(1)}, u32[]{:S(2)}, u32[]{:S(2)}) collective-permute-start(bf16[128,2048]{1,0:T(8,128)(2,1)} %get-tuple-element.22), channel_id=1, source_target_pairs={{32,0},{64,32},{96,64},{128,96},{160,128},{192,160},{224,192},{288... | collective-permute-start | bytes 1572872 | tf_op jit(solution)/shard_map/ppermute | solution.py:273
  78.5 35.8 %all-to-all-start.3 = ((bf16[16,136,128]{2,1,0:T(8,128)(2,1)}), bf16[16,136,128]{2,1,0:T(8,128)(2,1)S(1)}, u32[]{:S(2)}, u32[]{:S(2)}) async-start(bf16[16,136,128]{2,1,0:T(8,128)(2,1)} %broadcast_dynamic-update-slice_fusion), calls=%async_computation.3 | async-start | bytes 1114112 | tf_op jit(solution)/shard_map/all_to_all | solution.py:284
  87.4 21.5 %collective-permute-start.7 = (bf16[128,1024]{1,0:T(8,128)(2,1)S(1)}, bf16[128,1024]{1,0:T(8,128)(2,1)S(1)}, u32[]{:S(2)}, u32[]{:S(2)}) collective-permute-start(bf16[128,1024]{1,0:T(8,128)(2,1)S(1)} %get-tuple-element.32), channel_id=1, source_target_pairs={{224,256},{225,257},{256,224},{257,225},{226,258},{227,259},{258,2... | collective-permute-start | bytes 786440 | tf_op jit(solution)/shard_map/ppermute | solution.py:272
  92.0 21.3 %collective-permute-start.9 = (bf16[128,1024]{1,0:T(8,128)(2,1)S(1)}, bf16[128,1024]{1,0:T(8,128)(2,1)S(1)}, u32[]{:S(2)}, u32[]{:S(2)}) collective-permute-start(bf16[128,1024]{1,0:T(8,128)(2,1)S(1)} %collective-permute-done.8), channel_id=1, source_target_pairs={{481,256},{224,257},{1,224},{256,225},{483,258},{226,259},{3,226},... | collective-permute-start | bytes 786440 | tf_op jit(solution)/shard_map/ppermute | solution.py:275
  114.3 0.8 copy-start

commit v3 on v1

--- a/solution.py
+++ b/solution.py
@@ -197,32 +197,40 @@
 
     up = [(i, i + 1) for i in range(nseq - 1)]
     down = [(i + 1, i) for i in range(nseq - 1)]
-    table_out = jnp.broadcast_to(rel_bias.reshape(1, NREL), (nfsdp, NREL))
-    table = lax.all_to_all(table_out, "fsdp", 0, 0, tiled=True)
     own_kv = jnp.concatenate([key_rows[0], value_rows[0]], axis=1)
     left_kv = lax.ppermute(own_kv, "seq", up)
     right_kv = lax.ppermute(own_kv, "seq", down)
     own_sums = jnp.concatenate([summary_keys[0], summary_values[0]], axis=0)
     sums_out = jnp.broadcast_to(own_sums[None], (nseq, 2 * sum_rows, width))
     sums = lax.all_to_all(sums_out, "seq", 0, 0, tiled=True)
+    row = lax.broadcasted_iota(jnp.int32, (nfsdp, NREL), 0)
+    table = jnp.where(row == lax.axis_index("fsdp"), rel_bias.reshape(1, NREL), 0.0)
+    for step in range(int(math.log2(nfsdp))):
+        other = lax.ppermute(table, "fsdp", [(i, i ^ (1 << step)) for i in range(nfsdp)])
+        table = table + other
     place = jnp.stack([lax.axis_index("seq"), lax.axis_index("dp") * heads]).astype(jnp.int32)
 
     smem = pl.BlockSpec(memory_space=pltpu.SMEM)
     vmem = pl.BlockSpec(memory_space=pltpu.VMEM)
     shaped = jax.ShapeDtypeStruct
+
+    def near(value):
+        return pltpu.with_memory_space_constraint(value, pltpu.VMEM)
+
     attended, query_grad, to_left, to_right, own_grad, sum_grad, bias_part = pl.pallas_call(
         functools.partial(attention_kernel, heads, nblk, ndp),
         out_shape=(
             shaped((tok_rows, width), bf16),
             shaped((tok_rows, width), bf16),
-            shaped((BLK, 2 * width), bf16),
-            shaped((BLK, 2 * width), bf16),
-            shaped((BLK, 2 * width), f32),
-            shaped((nseq, 2 * heads * sum_rows + RIDE, HSIZE), bf16),
-            shaped((nfsdp * ndp, 1, BLK), f32),
+            pltpu.VMEM((BLK, 2 * width), bf16),
+            pltpu.VMEM((BLK, 2 * width), bf16),
+            pltpu.VMEM((BLK, 2 * width), f32),
+            pltpu.VMEM((nseq, 2 * heads * sum_rows + RIDE, HSIZE), bf16),
+            pltpu.VMEM((nfsdp * ndp, 1, BLK), f32),
         ),
         in_specs=[smem] * 4 + [vmem] * 7,
         out_specs=(vmem,) * 7,
+        compiler_params=pltpu.CompilerParams(vmem_limit_bytes=24 * 2**20),
         name="attention",
     )(
         place,
@@ -232,10 +240,10 @@
         summary_view.reshape(-1, 1),
         query_rows[0],
         out_grad[0],
-        own_kv,
-        left_kv,
-        right_kv,
-        sums,
+        near(own_kv),
+        near(left_kv),
+        near(right_kv),
+        near(sums),
     )
     bias_part = lax.all_to_all(bias_part, ("fsdp", "dp"), 0, 0, tiled=True)
     from_right = lax.ppermute(to_left, "seq", down)
@@ -262,8 +270,9 @@
         ),
         in_specs=[vmem],
         out_specs=(vmem,) * 3,
+        compiler_params=pltpu.CompilerParams(vmem_limit_bytes=16 * 2**20),
         name="finish",
-    )(sum_terms)
+    )(near(sum_terms))
     return (
         attended[None],
         query_grad[None],

time: 108 us -> 102 us (0.944)
  waiting for transfers between devices: 40.2 us -> 23.1 us
  starting transfers between devices: 46.2 us -> 60.8 us
  Pallas kernels: 9.73 us -> 7.15 us
  local copies, waits for them, and re-layouts: 8.2 us -> 6.98 us
    ppermute x0 -> x4, starting transfers between devices: none -> 21.5 us  [body(): lax.ppermute(table, 'fsdp', [(i, i ^ 1 << step) for i in range(nfsdp)])]
    ppermute x1, waiting for transfers between devices: 13.2 us -> 0.01 us  [body(): right_kv = lax.ppermute(own_kv, 'seq', down)]
    all_to_all x1 -> x0, starting transfers between devices: 10.4 us -> none  [body(): table = lax.all_to_all(table_out, 'fsdp', 0, 0, tiled=True)]
    all_to_all x1 -> x0, waiting for transfers between devices: 6.79 us -> none  [body(): table = lax.all_to_all(table_out, 'fsdp', 0, 0, tiled=True)]
    ppermute x0 -> x4, waiting for transfers between devices: none -> 3.9 us  [body(): lax.ppermute(table, 'fsdp', [(i, i ^ 1 << step) for i in range(nfsdp)])]
    all_to_all x1, starting transfers between devices: 3.96 us -> 7.71 us  [body(): bias_part = lax.all_to_all(bias_part, ('fsdp', 'dp'), 0, 0, tiled=True)]
    ppermute x1, waiting for transfers between devices: 15.6 us -> 13.6 us  [body(): from_right = lax.ppermute(to_left, 'seq', down)]
    pallas_call x1, Pallas kernels: 8 us -> 6.47 us  [body(): pl.pallas_call(functools.partial(attention_kernel, heads, nblk, ndp), out...]
  transfers between devices with their start and end apart: 8 -> 11, of which waited for: 6 -> 7; matrix products, arithmetic and copies ran while one was open for 5% -> 3% of each run, Pallas kernels for 0% -> 0%
where the time goes in v3:
time: 102 us; the launch traced here: 101 us
  starting transfers between devices  60.8 us (60%)
  waiting for transfers between devices  23.1 us (23%)
  Pallas kernels  7.15 us (7%)
  local copies, waits for them, and re-layouts  6.98 us (7%)
  other arithmetic  2.08 us (2%)
    ppermute x4, starting transfers between devices, body(): lax.ppermute(table, 'fsdp', [(i, i ^ 1 << step) for i in range(nfsdp)])  21.5 us
    ppermute x1, waiting for transfers between devices, body(): from_right = lax.ppermute(to_left, 'seq', down)  13.6 us
    all_to_all x1, starting transfers between devices, body(): sums = lax.all_to_all(sums_out, 'seq', 0, 0, tiled=True)  9.47 us
    all_to_all x1, starting transfers between devices, body(): bias_part = lax.all_to_all(bias_part, ('fsdp', 'dp'), 0, 0, tiled=True)  7.71 us
    all_to_all x1, starting transfers between devices, body(): sum_terms = lax.all_to_all(sum_grad, 'seq', 0, 0, tiled=True)  6.63 us
    pallas_call x1, Pallas kernels, body(): pl.pallas_call(functools.partial(attention_kernel, heads, nblk, ndp), out...  6.47 us
    ppermute x1, starting transfers between devices, body(): left_kv = lax.ppermute(own_kv, 'seq', up)  6.09 us
    unnamed x20, local copies, waits for them, and re-layouts  4.54 us
  transfers between devices with their start and end apart: 11, of which 7 were waited for; matrix products, arithmetic and copies ran while one was open for 3% of the time, Pallas kernels for 0%

profile of v3, /device:TPU:56, one launch (start us, length us, event | category | flops | bytes accessed | tf_op | source)
XLA Modules:
  0.0 100.9 jit_solution(15743535263424075366)
XLA Ops:
  0.6 0.7 pad_maximum_fusion.1
  1.4 0.9 broadcast_in_dim.47
  2.2 9.5 %all-to-all-start = ((bf16[16,16,1024]{2,1,0:T(8,128)(2,1)}), bf16[16,16,1024]{2,1,0:T(8,128)(2,1)S(1)}, u32[]{:S(2)}, u32[]{:S(2)}) async-start(bf16[16,16,1024]{2,1,0:T(8,128)(2,1)} %broadcast_in_dim.47), calls=%async_computation | async-start | bytes 1048576 | tf_op jit(solution)/shard_map/all_to_all | solution.py:205
  11.7 0.0 copy-start.7
  11.7 0.6 copy-done.7
  12.4 0.1 broadcast_select_fusion
  12.5 1.9 %collective-permute-start = (f32[16,4]{1,0:T(8,128)S(1)}, f32[16,4]{1,0:T(8,128)S(1)}, u32[]{:S(2)}, u32[]{:S(2)}) collective-permute-start(f32[16,4]{1,0:T(8,128)S(1)} %broadcast_select_fusion), channel_id=1, source_target_pairs={{0,2},{2,0},{4,6},{6,4},{8,10},{10,8},{12,14},{14,12},{16,18},{18,... | collective-permute-start | bytes 776 | tf_op jit(solution)/shard_map/ppermute | solution.py:209
  14.4 0.0 copy-done.5
  14.4 0.0 copy-done.6
  14.4 0.0 copy-start
  14.5 3.5 %collective-permute-start.5 = (bf16[128,2048]{1,0:T(8,128)(2,1)S(1)}, bf16[128,2048]{1,0:T(8,128)(2,1)S(1)}, u32[]{:S(2)}, u32[]{:S(2)}) collective-permute-start(bf16[128,2048]{1,0:T(8,128)(2,1)S(1)} %pad_maximum_fusion.own_kv), channel_id=1, source_target_pairs={{32,0},{64,32},{96,64},{128,96},{160,128},{192,160},{224,192},{256... | collective-permute-start | bytes 1572872 | tf_op jit(solution)/shard_map/ppermute | solution.py:202
  18.0 6.1 %collective-permute-start.4 = (bf16[128,2048]{1,0:T(8,128)(2,1)S(1)}, bf16[128,2048]{1,0:T(8,128)(2,1)S(1)}, u32[]{:S(2)}, u32[]{:S(2)}) collective-permute-start(bf16[128,2048]{1,0:T(8,128)(2,1)S(1)} %pad_maximum_fusion.own_kv), channel_id=1, source_target_pairs={{0,32},{32,64},{64,96},{96,128},{128,160},{160,192},{192,224},{224... | collective-permute-start | bytes 1572872 | tf_op jit(solution)/shard_map/ppermute | solution.py:201
  24.1 0.0 collective-permute-done
  24.1 0.1 fusion.6
  24.1 4.3 %collective-permute-start.1 = (f32[16,4]{1,0:T(8,128)S(1)}, f32[16,4]{1,0:T(8,128)S(1)}, u32[]{:S(2)}, u32[]{:S(2)}) collective-permute-start(f32[16,4]{1,0:T(8,128)S(1)} %fusion.6), channel_id=1, source_target_pairs={{0,4},{2,6},{4,0},{6,2},{8,12},{10,14},{12,8},{14,10},{16,20},{18,... | collective-permute-start | bytes 776 | tf_op jit(solution)/shard_map/ppermute | solution.py:209
  28.4 1.6 %collective-permute-done.1 = f32[16,4]{1,0:T(8,128)S(1)} collective-permute-done((f32[16,4]{1,0:T(8,128)S(1)}, f32[16,4]{1,0:T(8,128)S(1)}, u32[]{:S(2)}, u32[]{:S(2)}) %collective-permute-start.1) | collective-permute-done | bytes 288 | tf_op jit(solution)/shard_map/ppermute | solution.py:209
  30.0 0.1 fusion.11
  30.1 6.1 %collective-permute-start.2 = (f32[16,4]{1,0:T(8,128)S(1)}, f32[16,4]{1,0:T(8,128)S(1)}, u32[]{:S(2)}, u32[]{:S(2)}) collective-permute-start(f32[16,4]{1,0:T(8,128)S(1)} %fusion.11), channel_id=1, source_target_pairs={{0,8},{2,10},{4,12},{6,14},{8,0},{10,2},{12,4},{14,6},{16,24},{18,... | collective-permute-start | bytes 776 | tf_op jit(solution)/shard_map/ppermute | solution.py:209
  36.2 0.1 pad_add_fusion.place
  36.3 1.5 %collective-permute-done.2 = f32[16,4]{1,0:T(8,128)S(1)} collective-permute-done((f32[16,4]{1,0:T(8,128)S(1)}, f32[16,4]{1,0:T(8,128)S(1)}, u32[]{:S(2)}, u32[]{:S(2)}) %collective-permute-start.2) | collective-permute-done | bytes 288 | tf_op jit(solution)/shard_map/ppermute | solution.py:209
  37.8 9.3 %collective-permute-start.3 = (f32[16,4]{1,0:T(8,128)S(1)}, f32[16,4]{1,0:T(8,128)S(1)}, u32[]{:S(2)}, u32[]{:S(2)}) collective-permute-start(f32[16,4]{1,0:T(8,128)S(1)} %add.22), channel_id=1, source_target_pairs={{0,16},{2,18},{4,20},{6,22},{8,24},{10,26},{12,28},{14,30},{16,0},... | collective-permute-start | bytes 776 | tf_op jit(solution)/shard_map/ppermute | solution.py:209
  47.1 0.1 copy.19
  47.2 0.7 copy-done.9
  47.9 0.1 copy.18.sum_views
  48.0 0.8 collective-permute-done.3
  48.7 0.0 collective-permute-done.5.right_kv
  48.7 0.0 collective-permute-done.4.left_kv
  48.7 0.0 all-to-all-done.sums
  48.7 0.0 copy-start.2
  48.8 0.6 copy-done.2
  49.4 0.9 copy-done.1
  50.4 6.5 %attention.1 = (bf16[128,1024]{1,0:T(8,128)(2,1)}, bf16[128,1024]{1,0:T(8,128)(2,1)}, bf16[128,2048]{1,0:T(8,128)(2,1)S(1)}, bf16[128,2048]{1,0:T(8,128)(2,1)S(1...) custom-call(s32[2]{0:T(128)S(1)} %pad_add_fusion.place, s32[16,3]{1,0:T(8,128)S(1)} %bitcast.30, ...), custom_call_target="tpu_custom_call" | custom-call | tf_op jit(solution)/shard_map/attention/pallas_call | solution.py:220
  56.8 0.8 copy-done.3
  57.6 0.8 copy-done.4
  58.4 7.7 %all-to-all-start.1 = ((f32[32,1,128]{2,1,0:T(1,128)}), f32[32,1,128]{2,1,0:T(1,128)S(1)}, u32[]{:S(2)}, u32[]{:S(2)}) async-start(f32[32,1,128]{2,1,0:T(1,128)} %get-tuple-element.23), calls=%async_computation.1 | async-start | bytes 32768 | tf_op jit(solution)/shard_map/all_to_all | solution.py:248
  66.2 2.5 %collective-permute-start.6 = (bf16[128,2048]{1,0:T(8,128)(2,1)}, bf16[128,2048]{1,0:T(8,128)(2,1)S(1)}, u32[]{:S(2)}, u32[]{:S(2)}) collective-permute-start(bf16[128,2048]{1,0:T(8,128)(2,1)} %copy-done.4), channel_id=1, source_target_pairs={{0,32},{32,64},{64,96},{96,128},{128,160},{160,192},{192,224},{224... | collective-permute-start | bytes 1572872 | tf_op jit(solution)/shard_map/ppermute | solution.py:250
  68.7 3.3 %collective-permute-start.7 = (bf16[128,2048]{1,0:T(8,128)(2,1)}, bf16[128,2048]{1,0:T(8,128)(2,1)S(1)}, u32[]{:S(2)}, u32[]{:S(2)}) collective-permute-start(bf16[128,2048]{1,0:T(8,128)(2,1)} %copy-done.3), channel_id=1, source_target_pairs={{32,0},{64,32},{96,64},{128,96},{160,128},{192,160},{224,192},{256... | collective-permute-start | bytes 1572872 | tf_op jit(solution)/shard_map/ppermute | solution.py:249
  72.0 2.4 %all-to-all-done.1 = f32[32,1,128]{2,1,0:T(1,128)S(1)} async-done(((f32[32,1,128]{2,1,0:T(1,128)}), f32[32,1,128]{2,1,0:T(1,128)S(1)}, u32[]{:S(2)}, u32[]{:S(2)}) %all-to-all-start.1) | async-done | bytes 16416 | tf_op jit(solution)/shard_map/all_to_all | solution.py:248
  74.4 0.1 reduce_sum.11
  74.5 0.6 broadcast_dynamic-update-slice_fusion
  75.1 6.6 %all-to-all-start.2 = ((bf16[16,136,128]{2,1,0:T(8,128)(2,1)}), bf16[16,136,128]{2,1,0:T(8,128)(2,1)S(1)}, u32[]{:S(2)}, u32[]{:S(2)}) async-start(bf16[16,136,128]{2,1,0:T(8,128)(2,1)} %broadcast_dynamic-update-slice_fusion), calls=%async_computation.2 | async-start | bytes 1114112 | tf_op jit(solution)/shard_map/all_to_all | solution.py:259
  81.8 0.6 collective-permute-done.6
  82.4 13.6 %collective-permute-done.7 = bf16[128,2048]{1,0:T(8,128)(2,1)S(1)} collective-permute-done((bf16[128,2048]{1,0:T(8,128)(2,1)}, bf16[128,2048]{1,0:T(8,128)(2,1)S(1)}, u32[]{:S(2)}, u32[]{:S(2)}) %collective-permute-start.7) | collective-permute-done | bytes 524320 | tf_op jit(solution)/shard_map/ppermute | solution.py:249
  95.9 0.2 convert_add_fusion
  96.1 0.7 fusion.2
  96.8 0.8 fusion.1
  97.6 2.6 %all-to-all-done.2.terms = bf16[16,136,128]{2,1,0:T(8,128)(2,1)S(1)} async-done(((bf16[16,136,128]{2,1,0:T(8,128)(2,1)}), bf16[16,136,128]{2,1,0:T(8,128)(2,1)S(1)}, u32[]{:S(2)}, u32[]{:S(2)}) %all-to-all-start.2) | async-done | bytes 557088 | tf_op jit(solution)/shard_map/all_to_all | solution.py:259
  100.2 0.7 finish.1
  (15 shorter events, 0.1 us)
Async XLA Ops:
  2.2 12.1 %copy-start.5 = (bf16[1,128,1024]{2,1,0:T(8,128)(2,1)S(1)}, bf16[1,128,1024]{2,1,0:T(8,128)(2,1)}, u32[]{:S(2)}) copy-start(bf16[1,128,1024]{2,1,0:T(8,128)(2,1)} %param.12) | copy-start | bytes 786436
  2.2 12.1 %copy-start.6 = (bf16[1,128,1024]{2,1,0:T(8,128)(2,1)S(1)}, bf16[1,128,1024]{2,1,0:T(8,128)(2,1)}, u32[]{:S(2)}) copy-start(bf16[1,128,1024]{2,1,0:T(8,128)(2,1)} %param.11) | copy-start | bytes 786436
  2.2 46.5 %all-to-all-start = ((bf16[16,16,1024]{2,1,0:T(8,128)(2,1)}), bf16[16,16,1024]{2,1,0:T(8,128)(2,1)S(1)}, u32[]{:S(2)}, u32[]{:S(2)}) async-start(bf16[16,16,1024]{2,1,0:T(8,128)(2,1)} %broadcast_in_dim.47), calls=%async_computation | async-start | bytes 1048576 | tf_op jit(solution)/shard_map/all_to_all | solution.py:205
  11.7 0.7 copy-start.7
  12.5 11.6 %collective-permute-start = (f32[16,4]{1,0:T(8,128)S(1)}, f32[16,4]{1,0:T(8,128)S(1)}, u32[]{:S(2)}, u32[]{:S(2)}) collective-permute-start(f32[16,4]{1,0:T(8,128)S(1)} %broadcast_select_fusion), channel_id=1, source_target_pairs={{0,2},{2,0},{4,6},{6,4},{8,10},{10,8},{12,14},{14,12},{16,18},{18,... | collective-permute-start | bytes 776 | tf_op jit(solution)/shard_map/ppermute | solution.py:209
  14.4 34.4 %copy-start = (bf16[1,128,1024]{2,1,0:T(8,128)(2,1)S(1)}, bf16[1,128,1024]{2,1,0:T(8,128)(2,1)}, u32[]{:S(2)}) copy-start(bf16[1,128,1024]{2,1,0:T(8,128)(2,1)} %param.10) | copy-start | bytes 786436
  14.5 34.3 %collective-permute-start.5 = (bf16[128,2048]{1,0:T(8,128)(2,1)S(1)}, bf16[128,2048]{1,0:T(8,128)(2,1)S(1)}, u32[]{:S(2)}, u32[]{:S(2)}) collective-permute-start(bf16[128,2048]{1,0:T(8,128)(2,1)S(1)} %pad_maximum_fusion.own_kv), channel_id=1, source_target_pairs={{32,0},{64,32},{96,64},{128,96},{160,128},{192,160},{224,192},{256... | collective-permute-start | bytes 1572872 | tf_op jit(solution)/shard_map/ppermute | solution.py:202
  18.0 30.8 %collective-permute-start.4 = (bf16[128,2048]{1,0:T(8,128)(2,1)S(1)}, bf16[128,2048]{1,0:T(8,128)(2,1)S(1)}, u32[]{:S(2)}, u32[]{:S(2)}) collective-permute-start(bf16[128,2048]{1,0:T(8,128)(2,1)S(1)} %pad_maximum_fusion.own_kv), channel_id=1, source_target_pairs={{0,32},{32,64},{64,96},{96,128},{128,160},{160,192},{192,224},{224... | collective-permute-start | bytes 1572872 | tf_op jit(solution)/shard_map/ppermute | solution.py:201
  24.1 5.9 %collective-permute-start.1 = (f32[16,4]{1,0:T(8,128)S(1)}, f32[16,4]{1,0:T(8,128)S(1)}, u32[]{:S(2)}, u32[]{:S(2)}) collective-permute-start(f32[16,4]{1,0:T(8,128)S(1)} %fusion.6), channel_id=1, source_target_pairs={{0,4},{2,6},{4,0},{6,2},{8,12},{10,14},{12,8},{14,10},{16,20},{18,... | collective-permute-start | bytes 776 | tf_op jit(solution)/shard_map/ppermute | solution.py:209
  30.1 7.7 %collective-permute-start.2 = (f32[16,4]{1,0:T(8,128)S(1)}, f32[16,4]{1,0:T(8,128)S(1)}, u32[]{:S(2)}, u32[]{:S(2)}) collective-permute-start(f32[16,4]{1,0:T(8,128)S(1)} %fusion.11), channel_id=1, source_target_pairs={{0,8},{2,10},{4,12},{6,14},{8,0},{10,2},{12,4},{14,6},{16,24},{18,... | collective-permute-start | bytes 776 | tf_op jit(solution)/shard_map/ppermute | solution.py:209
  36.3 10.8 %copy-start.8 = (s32[1,16,3]{1,0,2:T(1,128)S(1)}, s32[1,16,3]{1,0,2:T(1,128)}, u32[]{:S(2)}) copy-start(s32[1,16,3]{1,0,2:T(1,128)} %param.17) | copy-start | bytes 580
  37.8 10.9 %collective-permute-start.3 = (f32[16,4]{1,0:T(8,128)S(1)}, f32[16,4]{1,0:T(8,128)S(1)}, u32[]{:S(2)}, u32[]{:S(2)}) collective-permute-start(f32[16,4]{1,0:T(8,128)S(1)} %add.22), channel_id=1, source_target_pairs={{0,16},{2,18},{4,20},{6,22},{8,24},{10,26},{12,28},{14,30},{16,0},... | collective-permute-start | bytes 776 | tf_op jit(solution)/shard_map/ppermute | solution.py:209
  47.2 0.7 copy-start.9
  48.7 0.7 copy-start.2
  49.4 0.9 copy-start.1
  56.8 0.8 copy-start.3
  57.6 0.8 copy-start.4
  58.4 16.0 %all-to-all-start.1 = ((f32[32,1,128]{2,1,0:T(1,128)}), f32[32,1,128]{2,1,0:T(1,128)S(1)}, u32[]{:S(2)}, u32[]{:S(2)}) async-start(f32[32,1,128]{2,1,0:T(1,128)} %get-tuple-element.23), calls=%async_computation.1 | async-start | bytes 32768 | tf_op jit(solution)/shard_map/all_to_all | solution.py:248
  66.2 16.2 %collective-permute-start.6 = (bf16[128,2048]{1,0:T(8,128)(2,1)}, bf16[128,2048]{1,0:T(8,128)(2,1)S(1)}, u32[]{:S(2)}, u32[]{:S(2)}) collective-permute-start(bf16[128,2048]{1,0:T(8,128)(2,1)} %copy-done.4), channel_id=1, source_target_pairs={{0,32},{32,64},{64,96},{96,128},{128,160},{160,192},{192,224},{224... | collective-permute-start | bytes 1572872 | tf_op jit(solution)/shard_map/ppermute | solution.py:250
  68.7 27.2 %collective-permute-start.7 = (bf16[128,2048]{1,0:T(8,128)(2,1)}, bf16[128,2048]{1,0:T(8,128)(2,1)S(1)}, u32[]{:S(2)}, u32[]{:S(2)}) collective-permute-start(bf16[128,2048]{1,0:T(8,128)(2,1)} %copy-done.3), channel_id=1, source_target_pairs={{32,0},{64,32},{96,64},{128,96},{160,128},{192,160},{224,192},{256... | collective-permute-start | bytes 1572872 | tf_op jit(solution)/shard_map/ppermute | solution.py:249
  75.1 25.0 %all-to-all-start.2 = ((bf16[16,136,128]{2,1,0:T(8,128)(2,1)}), bf16[16,136,128]{2,1,0:T(8,128)(2,1)S(1)}, u32[]{:S(2)}, u32[]{:S(2)}) async-start(bf16[16,136,128]{2,1,0:T(8,128)(2,1)} %broadcast_dynamic-update-slice_fusion), calls=%async_computation.2 | async-start | bytes 1114112 | tf_op jit(solution)/shard_map/all_to_all | solution.py:259

commit v4 on v3

--- a/solution.py
+++ b/solution.py
@@ -6,6 +6,7 @@
 from jax import lax
 from jax.experimental import pallas as pl
 from jax.experimental.pallas import tpu as pltpu
+from jax.sharding import Mesh
 from jax.sharding import PartitionSpec as P
 
 
@@ -45,6 +46,7 @@
 def attention_kernel(
     heads,
     nblk,
+    nfsdp,
     ndp,
     place,
     pattern,
@@ -62,7 +64,8 @@
     to_left,
     to_right,
     own_grad,
-    sum_grad,
+    sum_near,
+    sum_far,
     bias_part,
 ):
     block = place[0]
@@ -78,8 +81,13 @@
         jnp.where(pattern[block, slot] >= 0, jnp.float32(0.0), jnp.float32(NEG_FILL))
         for slot in range(3)
     ]
-    sum_class = view_class(own_view, sum_views[...])
-    count, rows = sums.shape[0], sums.shape[1] // 2
+    count, rows = sums.shape[0], sums.shape[1] // 4
+    part = count * rows
+    late_half = block >= nblk // 2
+    early_views, late_views = sum_views[:part], sum_views[part:]
+    near_views = lax.select(late_half, late_views, early_views)
+    far_views = lax.select(late_half, early_views, late_views)
+    sum_class = view_class(own_view, jnp.concatenate([near_views, far_views], axis=0))
     bias_part[...] = jnp.zeros_like(bias_part)
     class_row = lax.broadcasted_iota(jnp.int32, (8, BLK), 0)
     class_lane = lax.broadcasted_iota(jnp.int32, (8, BLK), 1)
@@ -93,7 +101,8 @@
                 left_kv[:, cols],
                 own_kv[:, cols],
                 right_kv[:, cols],
-                sums[:, :rows, cols].reshape(count * rows, HSIZE),
+                sums[:, :rows, cols].reshape(part, HSIZE),
+                sums[:, 2 * rows : 3 * rows, cols].reshape(part, HSIZE),
             ],
             axis=0,
         )
@@ -102,7 +111,8 @@
                 left_kv[:, late],
                 own_kv[:, late],
                 right_kv[:, late],
-                sums[:, rows:, cols].reshape(count * rows, HSIZE),
+                sums[:, rows : 2 * rows, cols].reshape(part, HSIZE),
+                sums[:, 3 * rows :, cols].reshape(part, HSIZE),
             ],
             axis=0,
         )
@@ -139,9 +149,10 @@
             own_grad[:, where] = terms[BLK : 2 * BLK]
             to_right[:, where] = terms[2 * BLK : 3 * BLK].astype(jnp.bfloat16)
             first = (index * heads + head) * rows
-            sum_grad[:, first : first + rows] = (
-                terms[3 * BLK :].astype(jnp.bfloat16).reshape(count, rows, HSIZE)
-            )
+            near = terms[3 * BLK : 3 * BLK + part]
+            far = terms[3 * BLK + part :].astype(jnp.bfloat16)
+            sum_near[:, first : first + rows] = near.reshape(count, rows, HSIZE)
+            sum_far[:, first : first + rows] = far.reshape(count, rows, HSIZE)
         slot_sums = [
             jnp.sum(score_grad[slot * BLK : (slot + 1) * BLK], axis=0, keepdims=True)
             for slot in range(3)
@@ -155,8 +166,24 @@
             tile = jnp.where(class_row == c, line, tile)
         totals = jnp.where(class_row == class_lane, jnp.sum(tile, axis=1, keepdims=True), 0.0)
         line = jnp.sum(totals, axis=0, keepdims=True)
-        for copy in range(ndp):
-            bias_part[ndp * (head_start + head) + copy] = line
+        for side in range(2):
+            for copy in range(ndp):
+                bias_part[(side * nfsdp + head_start + head) * ndp + copy] = line
+
+
+def merge_kernel(near, far, bias_part, merged):
+    size = near.shape[1]
+    merged[:, :size] = (near[...] + far[...].astype(jnp.float32)).astype(jnp.bfloat16)
+    rest = jnp.sum(bias_part[...], axis=0)
+    row = lax.broadcasted_iota(jnp.int32, (RIDE, BLK), 0)
+    ride = jnp.zeros((RIDE, BLK), jnp.float32)
+    for index in range(3):
+        piece = rest.astype(jnp.bfloat16).astype(jnp.float32)
+        ride = jnp.where(row == index, piece, ride)
+        rest = rest - piece
+    ride = ride.astype(jnp.bfloat16)
+    for i in range(near.shape[0]):
+        merged[i, size:] = ride
 
 
 def finish_kernel(heads, rows, terms, key_grad, value_grad, bias_grad):
@@ -188,7 +215,9 @@
 ):
     tok_rows, width = query_rows.shape[1:]
     heads = width // HSIZE
-    nseq = lax.axis_size("seq")
+    seq = ("half", "y")
+    half = lax.axis_size("y")
+    nseq = 2 * half
     nfsdp = lax.axis_size("fsdp")
     ndp = lax.axis_size("dp")
     nblk = block_view.shape[1]
@@ -197,18 +226,18 @@
 
     up = [(i, i + 1) for i in range(nseq - 1)]
     down = [(i + 1, i) for i in range(nseq - 1)]
+    swap = [(0, 1), (1, 0)]
     own_kv = jnp.concatenate([key_rows[0], value_rows[0]], axis=1)
-    left_kv = lax.ppermute(own_kv, "seq", up)
-    right_kv = lax.ppermute(own_kv, "seq", down)
+    left_kv = lax.ppermute(own_kv, seq, up)
+    right_kv = lax.ppermute(own_kv, seq, down)
+    table_out = jnp.broadcast_to(rel_bias.reshape(1, NREL), (nfsdp, NREL))
+    table = lax.all_to_all(table_out, "fsdp", 0, 0, tiled=True)
     own_sums = jnp.concatenate([summary_keys[0], summary_values[0]], axis=0)
-    sums_out = jnp.broadcast_to(own_sums[None], (nseq, 2 * sum_rows, width))
-    sums = lax.all_to_all(sums_out, "seq", 0, 0, tiled=True)
-    row = lax.broadcasted_iota(jnp.int32, (nfsdp, NREL), 0)
-    table = jnp.where(row == lax.axis_index("fsdp"), rel_bias.reshape(1, NREL), 0.0)
-    for step in range(int(math.log2(nfsdp))):
-        other = lax.ppermute(table, "fsdp", [(i, i ^ (1 << step)) for i in range(nfsdp)])
-        table = table + other
-    place = jnp.stack([lax.axis_index("seq"), lax.axis_index("dp") * heads]).astype(jnp.int32)
+    far_sums = lax.ppermute(own_sums, "half", swap)
+    sums_out = jnp.concatenate([own_sums, far_sums], axis=0)
+    sums_out = jnp.broadcast_to(sums_out[None], (half, 4 * sum_rows, width))
+    sums = lax.all_to_all(sums_out, "y", 0, 0, tiled=True)
+    place = jnp.stack([lax.axis_index(seq), lax.axis_index("dp") * heads]).astype(jnp.int32)
 
     smem = pl.BlockSpec(memory_space=pltpu.SMEM)
     vmem = pl.BlockSpec(memory_space=pltpu.VMEM)
@@ -217,20 +246,21 @@
     def near(value):
         return pltpu.with_memory_space_constraint(value, pltpu.VMEM)
 
-    attended, query_grad, to_left, to_right, own_grad, sum_grad, bias_part = pl.pallas_call(
-        functools.partial(attention_kernel, heads, nblk, ndp),
+    attended, query_grad, to_left, to_right, own_grad, near_terms, far_terms, bias_part = pl.pallas_call(
+        functools.partial(attention_kernel, heads, nblk, nfsdp, ndp),
         out_shape=(
             shaped((tok_rows, width), bf16),
             shaped((tok_rows, width), bf16),
-            pltpu.VMEM((BLK, 2 * width), bf16),
-            pltpu.VMEM((BLK, 2 * width), bf16),
-            pltpu.VMEM((BLK, 2 * width), f32),
-            pltpu.VMEM((nseq, 2 * heads * sum_rows + RIDE, HSIZE), bf16),
-            pltpu.VMEM((nfsdp * ndp, 1, BLK), f32),
+            shaped((BLK, 2 * width), bf16),
+            shaped((BLK, 2 * width), bf16),
+            shaped((BLK, 2 * width), f32),
+            shaped((half, 2 * heads * sum_rows, HSIZE), f32),
+            shaped((half, 2 * heads * sum_rows, HSIZE), bf16),
+            shaped((2 * nfsdp * ndp, 1, BLK), f32),
         ),
         in_specs=[smem] * 4 + [vmem] * 7,
-        out_specs=(vmem,) * 7,
-        compiler_params=pltpu.CompilerParams(vmem_limit_bytes=24 * 2**20),
+        out_specs=(vmem,) * 8,
+        compiler_params=pltpu.CompilerParams(vmem_limit_bytes=61 * 2**20),
         name="attention",
     )(
         place,
@@ -245,18 +275,19 @@
         near(right_kv),
         near(sums),
     )
-    bias_part = lax.all_to_all(bias_part, ("fsdp", "dp"), 0, 0, tiled=True)
-    from_right = lax.ppermute(to_left, "seq", down)
-    from_left = lax.ppermute(to_right, "seq", up)
-    rest = jnp.sum(bias_part, axis=0)
-    pieces = []
-    for _ in range(3):
-        pieces.append(lax.reduce_precision(rest, 8, 7))
-        rest = rest - pieces[-1]
-    rider = jnp.pad(jnp.concatenate(pieces, axis=0).astype(bf16), ((0, RIDE - 3), (0, 0)))
-    rider = jnp.broadcast_to(rider[None], (nseq, RIDE, BLK))
-    sum_grad = lax.dynamic_update_slice(sum_grad, rider, (0, 2 * heads * sum_rows, 0))
-    sum_terms = lax.all_to_all(sum_grad, "seq", 0, 0, tiled=True)
+    far_terms = lax.ppermute(far_terms, "half", swap)
+    bias_part = lax.all_to_all(bias_part, ("half", "fsdp", "dp"), 0, 0, tiled=True)
+    from_right = lax.ppermute(to_left, seq, down)
+    from_left = lax.ppermute(to_right, seq, up)
+    merged = pl.pallas_call(
+        merge_kernel,
+        out_shape=shaped((half, 2 * heads * sum_rows + RIDE, HSIZE), bf16),
+        in_specs=[vmem] * 3,
+        out_specs=vmem,
+        compiler_params=pltpu.CompilerParams(vmem_limit_bytes=16 * 2**20),
+        name="merge",
+    )(near_terms, near(far_terms), near(bias_part))
+    sum_terms = lax.all_to_all(merged, "y", 0, 0, tiled=True)
 
     grads = own_grad + from_left.astype(f32) + from_right.astype(f32)
     key_grad = (grads[:, :width] * SCALE).astype(bf16)
@@ -285,10 +316,12 @@
 
 
 def solution(mesh):
-    rows = P("fsdp", "seq", "dp")
+    nseq, nfsdp, ndp = (mesh.shape[name] for name in ("seq", "fsdp", "dp"))
+    split = Mesh(mesh.devices.reshape(2, nseq // 2, nfsdp, ndp), ("half", "y", "fsdp", "dp"))
+    rows = P("fsdp", ("half", "y"), "dp")
     return jax.shard_map(
         body,
-        mesh=mesh,
+        mesh=split,
         in_specs=(rows,) * 6
         + (P(None, "fsdp"), P("fsdp", None, None), P("fsdp", None), P("fsdp", None)),
         out_specs=(rows,) * 6 + (P(None, "fsdp"),),

time: 102 us -> 114 us (1.12)
  the two profiles are of different devices: /device:TPU:56 before, /device:TPU:1 now
where the time goes in v4:
time: 114 us
  starting transfers between devices  47.6 us (42%)
  waiting for transfers between devices  31.7 us (28%)
  blocking collectives  16.4 us (14%)
  Pallas kernels  8.91 us (8%)
  local copies, waits for them, and re-layouts  6.02 us (5%)
  other arithmetic  2.32 us (2%)
    all_to_all x1, blocking collectives, body(): lax.all_to_all(bias_part, ('half', 'fsdp', 'dp'), 0, 0, tiled=True)  16.4 us
    ppermute x1, waiting for transfers between devices, body(): right_kv = lax.ppermute(own_kv, seq, down)  15.3 us
    all_to_all x1, starting transfers between devices, body(): table = lax.all_to_all(table_out, 'fsdp', 0, 0, tiled=True)  11.3 us
    ppermute x1, starting transfers between devices, body(): far_terms = lax.ppermute(far_terms, 'half', swap)  10.3 us
    all_to_all x1, waiting for transfers between devices, body(): sum_terms = lax.all_to_all(merged, 'y', 0, 0, tiled=True)  9.46 us
    pallas_call x1, Pallas kernels, body(): pl.pallas_call(functools.partial(attention_kernel, heads, nblk, nfsdp, nd...  7.44 us
    all_to_all x1, starting transfers between devices, body(): sums = lax.all_to_all(sums_out, 'y', 0, 0, tiled=True)  6.95 us
    all_to_all x1, waiting for transfers between devices, body(): table = lax.all_to_all(table_out, 'fsdp', 0, 0, tiled=True)  6.93 us
  transfers between devices with their start and end apart: 9, of which 3 were waited for; matrix products, arithmetic and copies ran while one was open for 4% of the time, Pallas kernels for 1%

profile of v4, /device:TPU:1, one launch (start us, length us, event | category | flops | bytes accessed | tf_op | source)
XLA Modules:
  0.0 113.7 jit_solution(7894300359079561915)
XLA Ops:
  0.6 0.0 copy-start.9
  0.6 0.0 copy-start.5
  0.7 0.8 pad_maximum_fusion.2
  1.4 0.0 copy-start.4
  1.4 5.6 %collective-permute-start.2 = (bf16[16,1024]{1,0:T(8,128)(2,1)S(1)}, bf16[16,1024]{1,0:T(8,128)(2,1)S(1)}, u32[]{:S(2)}, u32[]{:S(2)}) collective-permute-start(bf16[16,1024]{1,0:T(8,128)(2,1)S(1)} %pad_maximum_fusion.2), channel_id=1, source_target_pairs={{0,256},{256,0},{1,257},{257,1},{2,258},{258,2},{3,259},{259,3},{4... | collective-permute-start | bytes 98312 | tf_op jit(solution)/shard_map/ppermute | solution.py:236
  7.0 0.0 copy-done.9
  7.0 0.6 broadcast_in_dim.32
  7.7 11.3 %all-to-all-start = ((f32[16,1,4]{2,1,0:T(1,128)}), f32[16,1,4]{2,1,0:T(1,128)S(1)}, u32[]{:S(2)}, u32[]{:S(2)}) async-start(f32[16,1,4]{2,1,0:T(1,128)} %broadcast_in_dim.32), calls=%async_computation | async-start | bytes 16384 | tf_op jit(solution)/shard_map/all_to_all | solution.py:234
  18.9 0.0 collective-permute-done.2
  18.9 0.0 copy-done.5
  19.0 0.0 copy-done.4
  19.0 6.9 %all-to-all-done = f32[16,1,4]{2,1,0:T(1,128)S(1)} async-done(((f32[16,1,4]{2,1,0:T(1,128)}), f32[16,1,4]{2,1,0:T(1,128)S(1)}, u32[]{:S(2)}, u32[]{:S(2)}) %all-to-all-start) | async-done | bytes 288 | tf_op jit(solution)/shard_map/all_to_all | solution.py:234
  25.9 0.0 copy-start.6
  25.9 0.9 broadcast_in_dim.33
  26.8 0.0 copy-done.6
  26.8 0.0 copy-start.2
  26.8 0.0 copy-start.3
  26.8 7.0 %all-to-all-start.1 = ((bf16[8,32,1024]{2,1,0:T(8,128)(2,1)}), bf16[8,32,1024]{2,1,0:T(8,128)(2,1)S(1)}, u32[]{:S(2)}, u32[]{:S(2)}) async-start(bf16[8,32,1024]{2,1,0:T(8,128)(2,1)} %broadcast_in_dim.33), calls=%async_computation.1 | async-start | bytes 1048576 | tf_op jit(solution)/shard_map/all_to_all | solution.py:239
  33.7 0.0 copy-done.2
  33.7 0.0 copy-done.3
  33.8 1.3 %collective-permute-start.1 = (bf16[128,2048]{1,0:T(8,128)(2,1)S(1)}, bf16[128,2048]{1,0:T(8,128)(2,1)S(1)}, u32[]{:S(2)}, u32[]{:S(2)}) collective-permute-start(bf16[128,2048]{1,0:T(8,128)(2,1)S(1)} %pad_maximum_fusion.own_kv), channel_id=1, source_target_pairs={{32,0},{64,32},{96,64},{128,96},{160,128},{192,160},{224,192},{256... | collective-permute-start | bytes 1572872 | tf_op jit(solution)/shard_map/ppermute | solution.py:232
  35.1 4.0 %collective-permute-start = (bf16[128,2048]{1,0:T(8,128)(2,1)S(1)}, bf16[128,2048]{1,0:T(8,128)(2,1)S(1)}, u32[]{:S(2)}, u32[]{:S(2)}) collective-permute-start(bf16[128,2048]{1,0:T(8,128)(2,1)S(1)} %pad_maximum_fusion.own_kv), channel_id=1, source_target_pairs={{0,32},{32,64},{64,96},{96,128},{128,160},{160,192},{192,224},{224... | collective-permute-start | bytes 1572872 | tf_op jit(solution)/shard_map/ppermute | solution.py:231
  39.1 0.0 copy-start.7
  39.1 0.7 copy-done.7
  39.8 0.7 copy.24
  40.5 0.7 copy-done.8
  41.1 0.7 copy.23.sum_views
  41.9 0.6 pad_add_fusion.place
  42.5 15.3 %collective-permute-done.1.right_kv = bf16[128,2048]{1,0:T(8,128)(2,1)S(1)} collective-permute-done((bf16[128,2048]{1,0:T(8,128)(2,1)S(1)}, bf16[128,2048]{1,0:T(8,128)(2,1)S(1)}, u32[]{:S(2)}, u32[]{:S(2)}) %collective-permute-start.1) | collective-permute-done | bytes 524320 | tf_op jit(solution)/shard_map/ppermute | solution.py:232
  57.7 0.0 collective-permute-done.left_kv
  57.7 0.0 all-to-all-done.1.sums
  57.7 7.4 %attention.1 = (bf16[128,1024]{1,0:T(8,128)(2,1)}, bf16[128,1024]{1,0:T(8,128)(2,1)}, bf16[128,2048]{1,0:T(8,128)(2,1)}, bf16[128,2048]{1,0:T(8,128)(2,1)}, f32[...) custom-call(s32[2]{0:T(128)} %pad_add_fusion.place, ...), custom_call_target="tpu_custom_call" | custom-call | tf_op jit(solution)/shard_map/attention/pallas_call | solution.py:249
  65.2 3.1 %collective-permute-start.3 = (bf16[128,2048]{1,0:T(8,128)(2,1)}, bf16[128,2048]{1,0:T(8,128)(2,1)S(1)}, u32[]{:S(2)}, u32[]{:S(2)}) collective-permute-start(bf16[128,2048]{1,0:T(8,128)(2,1)} %get-tuple-element.21), channel_id=1, source_target_pairs={{0,32},{32,64},{64,96},{96,128},{128,160},{160,192},{192,224},{224... | collective-permute-start | bytes 1572872 | tf_op jit(solution)/shard_map/ppermute | solution.py:281
  68.3 1.3 %collective-permute-start.4 = (bf16[128,2048]{1,0:T(8,128)(2,1)}, bf16[128,2048]{1,0:T(8,128)(2,1)S(1)}, u32[]{:S(2)}, u32[]{:S(2)}) collective-permute-start(bf16[128,2048]{1,0:T(8,128)(2,1)} %get-tuple-element.22), channel_id=1, source_target_pairs={{32,0},{64,32},{96,64},{128,96},{160,128},{192,160},{224,192},{256... | collective-permute-start | bytes 1572872 | tf_op jit(solution)/shard_map/ppermute | solution.py:280
  69.6 10.3 %collective-permute-start.5 = (bf16[8,128,128]{2,1,0:T(8,128)(2,1)}, bf16[8,128,128]{2,1,0:T(8,128)(2,1)S(1)}, u32[]{:S(2)}, u32[]{:S(2)}) collective-permute-start(bf16[8,128,128]{2,1,0:T(8,128)(2,1)} %get-tuple-element.24), channel_id=1, source_target_pairs={{0,256},{256,0},{1,257},{257,1},{2,258},{258,2},{3,259},{259,3},{4... | collective-permute-start | bytes 786440 | tf_op jit(solution)/shard_map/ppermute | solution.py:278
  79.9 16.4 %all_to_all.23.bias_part = f32[64,1,128]{2,1,0:T(1,128)S(1)} all-to-all(f32[64,1,128]{2,1,0:T(1,128)} %get-tuple-element.25), channel_id=1, replica_groups=mesh['half'=2,'y'=8,'fsdp'=16,'dp'=2] {'half','fsdp','dp'}, dimensions={0} | all-to-all | bytes 65536 | tf_op jit(solution)/shard_map/all_to_all | solution.py:279
  96.3 0.0 collective-permute-done.5.far
  96.3 1.0 copy-done
  97.3 0.8 merge.1
  98.2 3.8 %all-to-all-start.3 = ((bf16[8,136,128]{2,1,0:T(8,128)(2,1)}), bf16[8,136,128]{2,1,0:T(8,128)(2,1)S(1)}, u32[]{:S(2)}, u32[]{:S(2)}) async-start(bf16[8,136,128]{2,1,0:T(8,128)(2,1)} %merge.1), calls=%async_computation.3 | async-start | bytes 557056 | tf_op jit(solution)/shard_map/all_to_all | solution.py:290
  101.9 0.0 collective-permute-done.3
  102.0 0.0 collective-permute-done.4
  102.0 0.0 copy-done.1
  102.0 0.2 convert_add_fusion
  102.1 0.7 fusion.2
  102.9 0.8 fusion.1
  103.6 9.5 %all-to-all-done.3.terms = bf16[8,136,128]{2,1,0:T(8,128)(2,1)S(1)} async-done(((bf16[8,136,128]{2,1,0:T(8,128)(2,1)}), bf16[8,136,128]{2,1,0:T(8,128)(2,1)S(1)}, u32[]{:S(2)}, u32[]{:S(2)}) %all-to-all-start.3) | async-done | bytes 278560 | tf_op jit(solution)/shard_map/all_to_all | solution.py:290
  113.1 0.6 finish.1
  (5 shorter events, 0.0 us)
Async XLA Ops:
  0.6 6.4 %copy-start.9 = (f32[4,1]{0,1:T(1,128)S(1)}, f32[4,1]{0,1:T(1,128)}, u32[]{:S(2)}) copy-start(f32[4,1]{0,1:T(1,128)} %param.16) | copy-start | bytes 52
  0.6 18.3 %copy-start.5 = (bf16[1,8,1024]{2,1,0:T(8,128)(2,1)S(1)}, bf16[1,8,1024]{2,1,0:T(8,128)(2,1)}, u32[]{:S(2)}) copy-start(bf16[1,8,1024]{2,1,0:T(8,128)(2,1)} %param.13) | copy-start | bytes 49156
  1.4 17.5 %copy-start.4 = (bf16[1,8,1024]{2,1,0:T(8,128)(2,1)S(1)}, bf16[1,8,1024]{2,1,0:T(8,128)(2,1)}, u32[]{:S(2)}) copy-start(bf16[1,8,1024]{2,1,0:T(8,128)(2,1)} %param.14) | copy-start | bytes 49156
  1.4 17.5 %collective-permute-start.2 = (bf16[16,1024]{1,0:T(8,128)(2,1)S(1)}, bf16[16,1024]{1,0:T(8,128)(2,1)S(1)}, u32[]{:S(2)}, u32[]{:S(2)}) collective-permute-start(bf16[16,1024]{1,0:T(8,128)(2,1)S(1)} %pad_maximum_fusion.2), channel_id=1, source_target_pairs={{0,256},{256,0},{1,257},{257,1},{2,258},{258,2},{3,259},{259,3},{4... | collective-permute-start | bytes 98312 | tf_op jit(solution)/shard_map/ppermute | solution.py:236
  7.7 18.3 %all-to-all-start = ((f32[16,1,4]{2,1,0:T(1,128)}), f32[16,1,4]{2,1,0:T(1,128)S(1)}, u32[]{:S(2)}, u32[]{:S(2)}) async-start(f32[16,1,4]{2,1,0:T(1,128)} %broadcast_in_dim.32), calls=%async_computation | async-start | bytes 16384 | tf_op jit(solution)/shard_map/all_to_all | solution.py:234
  25.9 0.9 copy-start.6
  26.8 7.0 %copy-start.2 = (bf16[1,128,1024]{2,1,0:T(8,128)(2,1)S(1)}, bf16[1,128,1024]{2,1,0:T(8,128)(2,1)}, u32[]{:S(2)}) copy-start(bf16[1,128,1024]{2,1,0:T(8,128)(2,1)} %param.12) | copy-start | bytes 786436
  26.8 7.0 %copy-start.3 = (bf16[1,128,1024]{2,1,0:T(8,128)(2,1)S(1)}, bf16[1,128,1024]{2,1,0:T(8,128)(2,1)}, u32[]{:S(2)}) copy-start(bf16[1,128,1024]{2,1,0:T(8,128)(2,1)} %param.11) | copy-start | bytes 786436
  26.8 30.9 %all-to-all-start.1 = ((bf16[8,32,1024]{2,1,0:T(8,128)(2,1)}), bf16[8,32,1024]{2,1,0:T(8,128)(2,1)S(1)}, u32[]{:S(2)}, u32[]{:S(2)}) async-start(bf16[8,32,1024]{2,1,0:T(8,128)(2,1)} %broadcast_in_dim.33), calls=%async_computation.1 | async-start | bytes 1048576 | tf_op jit(solution)/shard_map/all_to_all | solution.py:239
  33.8 23.9 %collective-permute-start.1 = (bf16[128,2048]{1,0:T(8,128)(2,1)S(1)}, bf16[128,2048]{1,0:T(8,128)(2,1)S(1)}, u32[]{:S(2)}, u32[]{:S(2)}) collective-permute-start(bf16[128,2048]{1,0:T(8,128)(2,1)S(1)} %pad_maximum_fusion.own_kv), channel_id=1, source_target_pairs={{32,0},{64,32},{96,64},{128,96},{160,128},{192,160},{224,192},{256... | collective-permute-start | bytes 1572872 | tf_op jit(solution)/shard_map/ppermute | solution.py:232
  35.1 22.6 %collective-permute-start = (bf16[128,2048]{1,0:T(8,128)(2,1)S(1)}, bf16[128,2048]{1,0:T(8,128)(2,1)S(1)}, u32[]{:S(2)}, u32[]{:S(2)}) collective-permute-start(bf16[128,2048]{1,0:T(8,128)(2,1)S(1)} %pad_maximum_fusion.own_kv), channel_id=1, source_target_pairs={{0,32},{32,64},{64,96},{96,128},{128,160},{160,192},{192,224},{224... | collective-permute-start | bytes 1572872 | tf_op jit(solution)/shard_map/ppermute | solution.py:231
  39.1 0.7 copy-start.7
  40.5 0.7 copy-start.8
  65.2 36.8 %collective-permute-start.3 = (bf16[128,2048]{1,0:T(8,128)(2,1)}, bf16[128,2048]{1,0:T(8,128)(2,1)S(1)}, u32[]{:S(2)}, u32[]{:S(2)}) collective-permute-start(bf16[128,2048]{1,0:T(8,128)(2,1)} %get-tuple-element.21), channel_id=1, source_target_pairs={{0,32},{32,64},{64,96},{96,128},{128,160},{160,192},{192,224},{224... | collective-permute-start | bytes 1572872 | tf_op jit(solution)/shard_map/ppermute | solution.py:281
  68.3 33.7 %collective-permute-start.4 = (bf16[128,2048]{1,0:T(8,128)(2,1)}, bf16[128,2048]{1,0:T(8,128)(2,1)S(1)}, u32[]{:S(2)}, u32[]{:S(2)}) collective-permute-start(bf16[128,2048]{1,0:T(8,128)(2,1)} %get-tuple-element.22), channel_id=1, source_target_pairs={{32,0},{64,32},{96,64},{128,96},{160,128},{192,160},{224,192},{256... | collective-permute-start | bytes 1572872 | tf_op jit(solution)/shard_map/ppermute | solution.py:280
  69.6 26.7 %collective-permute-start.5 = (bf16[8,128,128]{2,1,0:T(8,128)(2,1)}, bf16[8,128,128]{2,1,0:T(8,128)(2,1)S(1)}, u32[]{:S(2)}, u32[]{:S(2)}) collective-permute-start(bf16[8,128,128]{2,1,0:T(8,128)(2,1)} %get-tuple-element.24), channel_id=1, source_target_pairs={{0,256},{256,0},{1,257},{257,1},{2,258},{258,2},{3,259},{259,3},{4... | collective-permute-start | bytes 786440 | tf_op jit(solution)/shard_map/ppermute | solution.py:278
  96.3 1.0 copy-start
  97.3 4.6 %copy-start.1 = (f32[128,2048]{1,0:T(8,128)S(1)}, f32[128,2048]{1,0:T(8,128)}, u32[]{:S(2)}) copy-start(f32[128,2048]{1,0:T(8,128)} %get-tuple-element.20) | copy-start | bytes 3145732
  98.2 14.9 %all-to-all-start.3 = ((bf16[8,136,128]{2,1,0:T(8,128)(2,1)}), bf16[8,136,128]{2,1,0:T(8,128)(2,1)S(1)}, u32[]{:S(2)}, u32[]{:S(2)}) async-start(bf16[8,136,128]{2,1,0:T(8,128)(2,1)} %merge.1), calls=%async_computation.3 | async-start | bytes 557056 | tf_op jit(solution)/shard_map/all_to_all | solution.py:290

commit v5 on v4

--- a/solution.py
+++ b/solution.py
@@ -81,9 +81,11 @@
         jnp.where(pattern[block, slot] >= 0, jnp.float32(0.0), jnp.float32(NEG_FILL))
         for slot in range(3)
     ]
-    count, rows = sums.shape[0], sums.shape[1] // 4
+    count, rows = sums.shape[0] // 2, sums.shape[1] // 2
     part = count * rows
     late_half = block >= nblk // 2
+    near_rows = pl.ds(jnp.where(late_half, count, 0), count)
+    far_rows = pl.ds(jnp.where(late_half, 0, count), count)
     early_views, late_views = sum_views[:part], sum_views[part:]
     near_views = lax.select(late_half, late_views, early_views)
     far_views = lax.select(late_half, early_views, late_views)
@@ -101,8 +103,8 @@
                 left_kv[:, cols],
                 own_kv[:, cols],
                 right_kv[:, cols],
-                sums[:, :rows, cols].reshape(part, HSIZE),
-                sums[:, 2 * rows : 3 * rows, cols].reshape(part, HSIZE),
+                sums[near_rows, :rows, cols].reshape(part, HSIZE),
+                sums[far_rows, :rows, cols].reshape(part, HSIZE),
             ],
             axis=0,
         )
@@ -111,8 +113,8 @@
                 left_kv[:, late],
                 own_kv[:, late],
                 right_kv[:, late],
-                sums[:, rows : 2 * rows, cols].reshape(part, HSIZE),
-                sums[:, 3 * rows :, cols].reshape(part, HSIZE),
+                sums[near_rows, rows:, cols].reshape(part, HSIZE),
+                sums[far_rows, rows:, cols].reshape(part, HSIZE),
             ],
             axis=0,
         )
@@ -230,13 +232,14 @@
     own_kv = jnp.concatenate([key_rows[0], value_rows[0]], axis=1)
     left_kv = lax.ppermute(own_kv, seq, up)
     right_kv = lax.ppermute(own_kv, seq, down)
-    table_out = jnp.broadcast_to(rel_bias.reshape(1, NREL), (nfsdp, NREL))
-    table = lax.all_to_all(table_out, "fsdp", 0, 0, tiled=True)
     own_sums = jnp.concatenate([summary_keys[0], summary_values[0]], axis=0)
-    far_sums = lax.ppermute(own_sums, "half", swap)
-    sums_out = jnp.concatenate([own_sums, far_sums], axis=0)
-    sums_out = jnp.broadcast_to(sums_out[None], (half, 4 * sum_rows, width))
-    sums = lax.all_to_all(sums_out, "y", 0, 0, tiled=True)
+    sums_out = jnp.broadcast_to(own_sums[None], (nseq, 2 * sum_rows, width))
+    sums = lax.all_to_all(sums_out, seq, 0, 0, tiled=True)
+    row = lax.broadcasted_iota(jnp.int32, (nfsdp, NREL), 0)
+    table = jnp.where(row == lax.axis_index("fsdp"), rel_bias.reshape(1, NREL), 0.0)
+    for step in range(int(math.log2(nfsdp))):
+        other = lax.ppermute(table, "fsdp", [(i, i ^ (1 << step)) for i in range(nfsdp)])
+        table = table + other
     place = jnp.stack([lax.axis_index(seq), lax.axis_index("dp") * heads]).astype(jnp.int32)
 
     smem = pl.BlockSpec(memory_space=pltpu.SMEM)

time: 114 us -> 107 us (0.939)
  waiting for transfers between devices: 31.7 us -> 11.8 us
  starting transfers between devices: 47.6 us -> 55.8 us
  blocking collectives: 16.4 us -> 19.9 us
    ppermute x1 -> x4, starting transfers between devices: 5.59 us -> 21.6 us  [body(): lax.ppermute(table, 'fsdp', [(i, i ^ 1 << step) for i in range(nfsdp)])]
    ppermute x1, waiting for transfers between devices: 15.3 us -> 0.01 us  [body(): right_kv = lax.ppermute(own_kv, seq, down)]
    all_to_all x2 -> x1, starting transfers between devices: 18.2 us -> 10.3 us  [body(): sums = lax.all_to_all(sums_out, seq, 0, 0, tiled=True)]
    all_to_all x2 -> x1, waiting for transfers between devices: 6.93 us -> 0.01 us  [body(): sums = lax.all_to_all(sums_out, seq, 0, 0, tiled=True)]
    all_to_all x1, blocking collectives: 16.4 us -> 19.9 us  [body(): lax.all_to_all(bias_part, ('half', 'fsdp', 'dp'), 0, 0, tiled=True)]
    ppermute x1 -> x4, waiting for transfers between devices: 0.01 us -> 2.49 us  [body(): lax.ppermute(table, 'fsdp', [(i, i ^ 1 << step) for i in range(nfsdp)])]
    unnamed x20 -> x14, local copies, waits for them, and re-layouts: 2.4 us -> 2.36 us
  transfers between devices with their start and end apart: 9 -> 11, of which waited for: 3 -> 4; matrix products, arithmetic and copies ran while one was open for 4% -> 4% of each run, Pallas kernels for 1% -> 1%
where the time goes in v5:
time: 107 us; the launch traced here: 106 us
  starting transfers between devices  55.8 us (52%)
  blocking collectives  19.9 us (19%)
  waiting for transfers between devices  11.8 us (11%)
  Pallas kernels  8.92 us (8%)
  local copies, waits for them, and re-layouts  5.39 us (5%)
  other arithmetic  3.17 us (3%)
    ppermute x4, starting transfers between devices, body(): lax.ppermute(table, 'fsdp', [(i, i ^ 1 << step) for i in range(nfsdp)])  21.6 us
    all_to_all x1, blocking collectives, body(): lax.all_to_all(bias_part, ('half', 'fsdp', 'dp'), 0, 0, tiled=True)  19.9 us
    all_to_all x1, starting transfers between devices, body(): sums = lax.all_to_all(sums_out, seq, 0, 0, tiled=True)  10.3 us
    ppermute x1, starting transfers between devices, body(): far_terms = lax.ppermute(far_terms, 'half', swap)  10.3 us
    all_to_all x1, waiting for transfers between devices, body(): sum_terms = lax.all_to_all(merged, 'y', 0, 0, tiled=True)  9.26 us
    pallas_call x1, Pallas kernels, body(): pl.pallas_call(functools.partial(attention_kernel, heads, nblk, nfsdp, nd...  7.44 us
    ppermute x1, starting transfers between devices, body(): left_kv = lax.ppermute(own_kv, seq, up)  4.02 us
    ppermute x1, starting transfers between devices, body(): from_left = lax.ppermute(to_right, seq, up)  3.53 us
  transfers between devices with their start and end apart: 11, of which 4 were waited for; matrix products, arithmetic and copies ran while one was open for 4% of the time, Pallas kernels for 1%

profile of v5, /device:TPU:1, one launch (start us, length us, event | category | flops | bytes accessed | tf_op | source)
XLA Modules:
  0.0 105.8 jit_solution(4865238339668245968)
XLA Ops:
  0.6 0.7 pad_maximum_fusion.1
  1.4 0.9 broadcast_in_dim.41
  2.2 0.0 copy-start.2
  2.2 0.0 copy-start.3
  2.2 10.3 %all-to-all-start = ((bf16[16,16,1024]{2,1,0:T(8,128)(2,1)}), bf16[16,16,1024]{2,1,0:T(8,128)(2,1)S(1)}, u32[]{:S(2)}, u32[]{:S(2)}) async-start(bf16[16,16,1024]{2,1,0:T(8,128)(2,1)} %broadcast_in_dim.41), calls=%async_computation | async-start | bytes 1048576 | tf_op jit(solution)/shard_map/all_to_all | solution.py:237
  12.6 0.0 copy-done.2
  12.6 0.0 copy-done.3
  12.6 1.3 %collective-permute-start.5 = (bf16[128,2048]{1,0:T(8,128)(2,1)S(1)}, bf16[128,2048]{1,0:T(8,128)(2,1)S(1)}, u32[]{:S(2)}, u32[]{:S(2)}) collective-permute-start(bf16[128,2048]{1,0:T(8,128)(2,1)S(1)} %pad_maximum_fusion.own_kv), channel_id=1, source_target_pairs={{32,0},{64,32},{96,64},{128,96},{160,128},{192,160},{224,192},{256... | collective-permute-start | bytes 1572872 | tf_op jit(solution)/shard_map/ppermute | solution.py:234
  13.9 4.0 %collective-permute-start.4 = (bf16[128,2048]{1,0:T(8,128)(2,1)S(1)}, bf16[128,2048]{1,0:T(8,128)(2,1)S(1)}, u32[]{:S(2)}, u32[]{:S(2)}) collective-permute-start(bf16[128,2048]{1,0:T(8,128)(2,1)S(1)} %pad_maximum_fusion.own_kv), channel_id=1, source_target_pairs={{0,32},{32,64},{64,96},{96,128},{128,160},{160,192},{192,224},{224... | collective-permute-start | bytes 1572872 | tf_op jit(solution)/shard_map/ppermute | solution.py:233
  18.0 0.0 copy-start.4
  18.0 0.6 copy-done.4
  18.7 0.1 broadcast_select_fusion
  18.7 3.4 %collective-permute-start = (f32[16,4]{1,0:T(8,128)S(1)}, f32[16,4]{1,0:T(8,128)S(1)}, u32[]{:S(2)}, u32[]{:S(2)}) collective-permute-start(f32[16,4]{1,0:T(8,128)S(1)} %broadcast_select_fusion), channel_id=1, source_target_pairs={{0,2},{2,0},{4,6},{6,4},{8,10},{10,8},{12,14},{14,12},{16,18},{18,... | collective-permute-start | bytes 776 | tf_op jit(solution)/shard_map/ppermute | solution.py:241
  22.2 0.8 collective-permute-done
  23.0 0.1 fusion.3
  23.0 4.0 %collective-permute-start.1 = (f32[16,4]{1,0:T(8,128)S(1)}, f32[16,4]{1,0:T(8,128)S(1)}, u32[]{:S(2)}, u32[]{:S(2)}) collective-permute-start(f32[16,4]{1,0:T(8,128)S(1)} %fusion.3), channel_id=1, source_target_pairs={{0,4},{2,6},{4,0},{6,2},{8,12},{10,14},{12,8},{14,10},{16,20},{18,... | collective-permute-start | bytes 776 | tf_op jit(solution)/shard_map/ppermute | solution.py:241
  27.0 1.3 %collective-permute-done.1 = f32[16,4]{1,0:T(8,128)S(1)} collective-permute-done((f32[16,4]{1,0:T(8,128)S(1)}, f32[16,4]{1,0:T(8,128)S(1)}, u32[]{:S(2)}, u32[]{:S(2)}) %collective-permute-start.1) | collective-permute-done | bytes 288 | tf_op jit(solution)/shard_map/ppermute | solution.py:241
  28.3 0.1 fusion.4
  28.4 5.8 %collective-permute-start.2 = (f32[16,4]{1,0:T(8,128)S(1)}, f32[16,4]{1,0:T(8,128)S(1)}, u32[]{:S(2)}, u32[]{:S(2)}) collective-permute-start(f32[16,4]{1,0:T(8,128)S(1)} %fusion.4), channel_id=1, source_target_pairs={{0,8},{2,10},{4,12},{6,14},{8,0},{10,2},{12,4},{14,6},{16,24},{18,... | collective-permute-start | bytes 776 | tf_op jit(solution)/shard_map/ppermute | solution.py:241
  34.2 0.6 pad_add_fusion.place
  34.9 0.4 collective-permute-done.2
  35.3 8.4 %collective-permute-start.3 = (f32[16,4]{1,0:T(8,128)S(1)}, f32[16,4]{1,0:T(8,128)S(1)}, u32[]{:S(2)}, u32[]{:S(2)}) collective-permute-start(f32[16,4]{1,0:T(8,128)S(1)} %add.24), channel_id=1, source_target_pairs={{0,16},{2,18},{4,20},{6,22},{8,24},{10,26},{12,28},{14,30},{16,0},... | collective-permute-start | bytes 776 | tf_op jit(solution)/shard_map/ppermute | solution.py:241
  43.7 0.0 copy-done.5
  43.7 0.7 copy.19
  44.4 0.7 copy-done.6
  45.0 0.7 copy.18.sum_views
  45.8 0.0 collective-permute-done.3
  45.8 0.6 add.25.table
  46.4 0.0 collective-permute-done.5.right_kv
  46.4 0.0 collective-permute-done.4.left_kv
  46.4 0.0 all-to-all-done.sums
  46.4 7.4 %attention.1 = (bf16[128,1024]{1,0:T(8,128)(2,1)}, bf16[128,1024]{1,0:T(8,128)(2,1)}, bf16[128,2048]{1,0:T(8,128)(2,1)}, bf16[128,2048]{1,0:T(8,128)(2,1)}, f32[...) custom-call(s32[2]{0:T(128)} %pad_add_fusion.place, ...), custom_call_target="tpu_custom_call" | custom-call | tf_op jit(solution)/shard_map/attention/pallas_call | solution.py:252
  53.8 3.5 %collective-permute-start.6 = (bf16[128,2048]{1,0:T(8,128)(2,1)}, bf16[128,2048]{1,0:T(8,128)(2,1)S(1)}, u32[]{:S(2)}, u32[]{:S(2)}) collective-permute-start(bf16[128,2048]{1,0:T(8,128)(2,1)} %get-tuple-element.21), channel_id=1, source_target_pairs={{0,32},{32,64},{64,96},{96,128},{128,160},{160,192},{192,224},{224... | collective-permute-start | bytes 1572872 | tf_op jit(solution)/shard_map/ppermute | solution.py:284
  57.4 1.3 %collective-permute-start.7 = (bf16[128,2048]{1,0:T(8,128)(2,1)}, bf16[128,2048]{1,0:T(8,128)(2,1)S(1)}, u32[]{:S(2)}, u32[]{:S(2)}) collective-permute-start(bf16[128,2048]{1,0:T(8,128)(2,1)} %get-tuple-element.22), channel_id=1, source_target_pairs={{32,0},{64,32},{96,64},{128,96},{160,128},{192,160},{224,192},{256... | collective-permute-start | bytes 1572872 | tf_op jit(solution)/shard_map/ppermute | solution.py:283
  58.7 10.3 %collective-permute-start.8 = (bf16[8,128,128]{2,1,0:T(8,128)(2,1)}, bf16[8,128,128]{2,1,0:T(8,128)(2,1)S(1)}, u32[]{:S(2)}, u32[]{:S(2)}) collective-permute-start(bf16[8,128,128]{2,1,0:T(8,128)(2,1)} %get-tuple-element.24), channel_id=1, source_target_pairs={{0,256},{256,0},{1,257},{257,1},{2,258},{258,2},{3,259},{259,3},{4... | collective-permute-start | bytes 786440 | tf_op jit(solution)/shard_map/ppermute | solution.py:281
  69.0 19.9 %all_to_all.15.bias_part = f32[64,1,128]{2,1,0:T(1,128)S(1)} all-to-all(f32[64,1,128]{2,1,0:T(1,128)} %get-tuple-element.25), channel_id=1, replica_groups=mesh['half'=2,'y'=8,'fsdp'=16,'dp'=2] {'half','fsdp','dp'}, dimensions={0} | all-to-all | bytes 65536 | tf_op jit(solution)/shard_map/all_to_all | solution.py:282
  88.9 0.0 collective-permute-done.8.far
  88.9 1.0 copy-done
  89.9 0.8 merge.1
  90.8 3.4 %all-to-all-start.2 = ((bf16[8,136,128]{2,1,0:T(8,128)(2,1)}), bf16[8,136,128]{2,1,0:T(8,128)(2,1)S(1)}, u32[]{:S(2)}, u32[]{:S(2)}) async-start(bf16[8,136,128]{2,1,0:T(8,128)(2,1)} %merge.1), calls=%async_computation.2 | async-start | bytes 557056 | tf_op jit(solution)/shard_map/all_to_all | solution.py:293
  94.2 0.0 collective-permute-done.6
  94.2 0.0 collective-permute-done.7
  94.2 0.0 copy-done.1
  94.2 0.2 convert_add_fusion
  94.4 0.7 fusion.2
  95.1 0.8 fusion.1
  95.9 9.3 %all-to-all-done.2.terms = bf16[8,136,128]{2,1,0:T(8,128)(2,1)S(1)} async-done(((bf16[8,136,128]{2,1,0:T(8,128)(2,1)}), bf16[8,136,128]{2,1,0:T(8,128)(2,1)S(1)}, u32[]{:S(2)}, u32[]{:S(2)}) %all-to-all-start.2) | async-done | bytes 278560 | tf_op jit(solution)/shard_map/all_to_all | solution.py:293
  105.2 0.6 finish.1
  (7 shorter events, 0.1 us)
Async XLA Ops:
  2.2 10.3 %copy-start.2 = (bf16[1,128,1024]{2,1,0:T(8,128)(2,1)S(1)}, bf16[1,128,1024]{2,1,0:T(8,128)(2,1)}, u32[]{:S(2)}) copy-start(bf16[1,128,1024]{2,1,0:T(8,128)(2,1)} %param.12) | copy-start | bytes 786436
  2.2 10.4 %copy-start.3 = (bf16[1,128,1024]{2,1,0:T(8,128)(2,1)S(1)}, bf16[1,128,1024]{2,1,0:T(8,128)(2,1)}, u32[]{:S(2)}) copy-start(bf16[1,128,1024]{2,1,0:T(8,128)(2,1)} %param.11) | copy-start | bytes 786436
  2.2 44.2 %all-to-all-start = ((bf16[16,16,1024]{2,1,0:T(8,128)(2,1)}), bf16[16,16,1024]{2,1,0:T(8,128)(2,1)S(1)}, u32[]{:S(2)}, u32[]{:S(2)}) async-start(bf16[16,16,1024]{2,1,0:T(8,128)(2,1)} %broadcast_in_dim.41), calls=%async_computation | async-start | bytes 1048576 | tf_op jit(solution)/shard_map/all_to_all | solution.py:237
  12.6 33.7 %collective-permute-start.5 = (bf16[128,2048]{1,0:T(8,128)(2,1)S(1)}, bf16[128,2048]{1,0:T(8,128)(2,1)S(1)}, u32[]{:S(2)}, u32[]{:S(2)}) collective-permute-start(bf16[128,2048]{1,0:T(8,128)(2,1)S(1)} %pad_maximum_fusion.own_kv), channel_id=1, source_target_pairs={{32,0},{64,32},{96,64},{128,96},{160,128},{192,160},{224,192},{256... | collective-permute-start | bytes 1572872 | tf_op jit(solution)/shard_map/ppermute | solution.py:234
  13.9 32.5 %collective-permute-start.4 = (bf16[128,2048]{1,0:T(8,128)(2,1)S(1)}, bf16[128,2048]{1,0:T(8,128)(2,1)S(1)}, u32[]{:S(2)}, u32[]{:S(2)}) collective-permute-start(bf16[128,2048]{1,0:T(8,128)(2,1)S(1)} %pad_maximum_fusion.own_kv), channel_id=1, source_target_pairs={{0,32},{32,64},{64,96},{96,128},{128,160},{160,192},{192,224},{224... | collective-permute-start | bytes 1572872 | tf_op jit(solution)/shard_map/ppermute | solution.py:233
  18.0 0.7 copy-start.4
  18.7 4.2 %collective-permute-start = (f32[16,4]{1,0:T(8,128)S(1)}, f32[16,4]{1,0:T(8,128)S(1)}, u32[]{:S(2)}, u32[]{:S(2)}) collective-permute-start(f32[16,4]{1,0:T(8,128)S(1)} %broadcast_select_fusion), channel_id=1, source_target_pairs={{0,2},{2,0},{4,6},{6,4},{8,10},{10,8},{12,14},{14,12},{16,18},{18,... | collective-permute-start | bytes 776 | tf_op jit(solution)/shard_map/ppermute | solution.py:241
  23.0 5.3 %collective-permute-start.1 = (f32[16,4]{1,0:T(8,128)S(1)}, f32[16,4]{1,0:T(8,128)S(1)}, u32[]{:S(2)}, u32[]{:S(2)}) collective-permute-start(f32[16,4]{1,0:T(8,128)S(1)} %fusion.3), channel_id=1, source_target_pairs={{0,4},{2,6},{4,0},{6,2},{8,12},{10,14},{12,8},{14,10},{16,20},{18,... | collective-permute-start | bytes 776 | tf_op jit(solution)/shard_map/ppermute | solution.py:241
  28.4 6.8 %collective-permute-start.2 = (f32[16,4]{1,0:T(8,128)S(1)}, f32[16,4]{1,0:T(8,128)S(1)}, u32[]{:S(2)}, u32[]{:S(2)}) collective-permute-start(f32[16,4]{1,0:T(8,128)S(1)} %fusion.4), channel_id=1, source_target_pairs={{0,8},{2,10},{4,12},{6,14},{8,0},{10,2},{12,4},{14,6},{16,24},{18,... | collective-permute-start | bytes 776 | tf_op jit(solution)/shard_map/ppermute | solution.py:241
  34.9 8.8 %copy-start.5 = (s32[1,16,3]{1,0,2:T(1,128)S(1)}, s32[1,16,3]{1,0,2:T(1,128)}, u32[]{:S(2)}) copy-start(s32[1,16,3]{1,0,2:T(1,128)} %param.17) | copy-start | bytes 580
  35.3 10.5 %collective-permute-start.3 = (f32[16,4]{1,0:T(8,128)S(1)}, f32[16,4]{1,0:T(8,128)S(1)}, u32[]{:S(2)}, u32[]{:S(2)}) collective-permute-start(f32[16,4]{1,0:T(8,128)S(1)} %add.24), channel_id=1, source_target_pairs={{0,16},{2,18},{4,20},{6,22},{8,24},{10,26},{12,28},{14,30},{16,0},... | collective-permute-start | bytes 776 | tf_op jit(solution)/shard_map/ppermute | solution.py:241
  44.4 0.7 copy-start.6
  53.8 40.4 %collective-permute-start.6 = (bf16[128,2048]{1,0:T(8,128)(2,1)}, bf16[128,2048]{1,0:T(8,128)(2,1)S(1)}, u32[]{:S(2)}, u32[]{:S(2)}) collective-permute-start(bf16[128,2048]{1,0:T(8,128)(2,1)} %get-tuple-element.21), channel_id=1, source_target_pairs={{0,32},{32,64},{64,96},{96,128},{128,160},{160,192},{192,224},{224... | collective-permute-start | bytes 1572872 | tf_op jit(solution)/shard_map/ppermute | solution.py:284
  57.4 36.8 %collective-permute-start.7 = (bf16[128,2048]{1,0:T(8,128)(2,1)}, bf16[128,2048]{1,0:T(8,128)(2,1)S(1)}, u32[]{:S(2)}, u32[]{:S(2)}) collective-permute-start(bf16[128,2048]{1,0:T(8,128)(2,1)} %get-tuple-element.22), channel_id=1, source_target_pairs={{32,0},{64,32},{96,64},{128,96},{160,128},{192,160},{224,192},{256... | collective-permute-start | bytes 1572872 | tf_op jit(solution)/shard_map/ppermute | solution.py:283
  58.7 30.2 %collective-permute-start.8 = (bf16[8,128,128]{2,1,0:T(8,128)(2,1)}, bf16[8,128,128]{2,1,0:T(8,128)(2,1)S(1)}, u32[]{:S(2)}, u32[]{:S(2)}) collective-permute-start(bf16[8,128,128]{2,1,0:T(8,128)(2,1)} %get-tuple-element.24), channel_id=1, source_target_pairs={{0,256},{256,0},{1,257},{257,1},{2,258},{258,2},{3,259},{259,3},{4... | collective-permute-start | bytes 786440 | tf_op jit(solution)/shard_map/ppermute | solution.py:281
  88.9 1.0 copy-start
  89.9 4.3 %copy-start.1 = (f32[128,2048]{1,0:T(8,128)S(1)}, f32[128,2048]{1,0:T(8,128)}, u32[]{:S(2)}) copy-start(f32[128,2048]{1,0:T(8,128)} %get-tuple-element.20) | copy-start | bytes 3145732
  90.8 14.4 %all-to-all-start.2 = ((bf16[8,136,128]{2,1,0:T(8,128)(2,1)}), bf16[8,136,128]{2,1,0:T(8,128)(2,1)S(1)}, u32[]{:S(2)}, u32[]{:S(2)}) async-start(bf16[8,136,128]{2,1,0:T(8,128)(2,1)} %merge.1), calls=%async_computation.2 | async-start | bytes 557056 | tf_op jit(solution)/shard_map/all_to_all | solution.py:293

commit v6 on v5

--- a/solution.py
+++ b/solution.py
@@ -237,8 +237,10 @@
     sums = lax.all_to_all(sums_out, seq, 0, 0, tiled=True)
     row = lax.broadcasted_iota(jnp.int32, (nfsdp, NREL), 0)
     table = jnp.where(row == lax.axis_index("fsdp"), rel_bias.reshape(1, NREL), 0.0)
-    for step in range(int(math.log2(nfsdp))):
-        other = lax.ppermute(table, "fsdp", [(i, i ^ (1 << step)) for i in range(nfsdp)])
+    bits = list(range(int(math.log2(nfsdp))))
+    bits.insert(1, bits.pop())
+    for bit in bits:
+        other = lax.ppermute(table, "fsdp", [(i, i ^ (1 << bit)) for i in range(nfsdp)])
         table = table + other
     place = jnp.stack([lax.axis_index(seq), lax.axis_index("dp") * heads]).astype(jnp.int32)
 

time: 107 us -> 107 us (level)
  no operation moved by 1% of the time
where the time goes in v6:
time: 107 us; the launch traced here: 106 us
  starting transfers between devices  55.4 us (52%)
  blocking collectives  20.4 us (19%)
  waiting for transfers between devices  11.8 us (11%)
  Pallas kernels  8.92 us (8%)
  local copies, waits for them, and re-layouts  5.39 us (5%)
  other arithmetic  3.17 us (3%)
    ppermute x4, starting transfers between devices, body(): lax.ppermute(table, 'fsdp', [(i, i ^ 1 << bit) for i in range(nfsdp)])  21.5 us
    all_to_all x1, blocking collectives, body(): lax.all_to_all(bias_part, ('half', 'fsdp', 'dp'), 0, 0, tiled=True)  20.4 us
    all_to_all x1, starting transfers between devices, body(): sums = lax.all_to_all(sums_out, seq, 0, 0, tiled=True)  10.3 us
    ppermute x1, starting transfers between devices, body(): far_terms = lax.ppermute(far_terms, 'half', swap)  10.2 us
    all_to_all x1, waiting for transfers between devices, body(): sum_terms = lax.all_to_all(merged, 'y', 0, 0, tiled=True)  9.27 us
    pallas_call x1, Pallas kernels, body(): pl.pallas_call(functools.partial(attention_kernel, heads, nblk, nfsdp, nd...  7.44 us
    ppermute x1, starting transfers between devices, body(): left_kv = lax.ppermute(own_kv, seq, up)  4.02 us
    all_to_all x1, starting transfers between devices, body(): sum_terms = lax.all_to_all(merged, 'y', 0, 0, tiled=True)  3.42 us
  transfers between devices with their start and end apart: 11, of which 4 were waited for; matrix products, arithmetic and copies ran while one was open for 4% of the time, Pallas kernels for 1%

profile of v6, /device:TPU:1, one launch (start us, length us, event | category | flops | bytes accessed | tf_op | source)
XLA Modules:
  0.0 105.8 jit_solution(10726242053291040254)
XLA Ops:
  0.6 0.7 pad_maximum_fusion.1
  1.4 0.9 broadcast_in_dim.41
  2.2 0.0 copy-start.2
  2.2 0.0 copy-start.3
  2.2 10.3 %all-to-all-start = ((bf16[16,16,1024]{2,1,0:T(8,128)(2,1)}), bf16[16,16,1024]{2,1,0:T(8,128)(2,1)S(1)}, u32[]{:S(2)}, u32[]{:S(2)}) async-start(bf16[16,16,1024]{2,1,0:T(8,128)(2,1)} %broadcast_in_dim.41), calls=%async_computation | async-start | bytes 1048576 | tf_op jit(solution)/shard_map/all_to_all | solution.py:237
  12.6 0.0 copy-done.2
  12.6 0.0 copy-done.3
  12.6 1.3 %collective-permute-start.5 = (bf16[128,2048]{1,0:T(8,128)(2,1)S(1)}, bf16[128,2048]{1,0:T(8,128)(2,1)S(1)}, u32[]{:S(2)}, u32[]{:S(2)}) collective-permute-start(bf16[128,2048]{1,0:T(8,128)(2,1)S(1)} %pad_maximum_fusion.own_kv), channel_id=1, source_target_pairs={{32,0},{64,32},{96,64},{128,96},{160,128},{192,160},{224,192},{256... | collective-permute-start | bytes 1572872 | tf_op jit(solution)/shard_map/ppermute | solution.py:234
  13.9 4.0 %collective-permute-start.4 = (bf16[128,2048]{1,0:T(8,128)(2,1)S(1)}, bf16[128,2048]{1,0:T(8,128)(2,1)S(1)}, u32[]{:S(2)}, u32[]{:S(2)}) collective-permute-start(bf16[128,2048]{1,0:T(8,128)(2,1)S(1)} %pad_maximum_fusion.own_kv), channel_id=1, source_target_pairs={{0,32},{32,64},{64,96},{96,128},{128,160},{160,192},{192,224},{224... | collective-permute-start | bytes 1572872 | tf_op jit(solution)/shard_map/ppermute | solution.py:233
  18.0 0.0 copy-start.4
  18.0 0.6 copy-done.4
  18.7 0.1 broadcast_select_fusion
  18.7 3.4 %collective-permute-start = (f32[16,4]{1,0:T(8,128)S(1)}, f32[16,4]{1,0:T(8,128)S(1)}, u32[]{:S(2)}, u32[]{:S(2)}) collective-permute-start(f32[16,4]{1,0:T(8,128)S(1)} %broadcast_select_fusion), channel_id=1, source_target_pairs={{0,2},{2,0},{4,6},{6,4},{8,10},{10,8},{12,14},{14,12},{16,18},{18,... | collective-permute-start | bytes 776 | tf_op jit(solution)/shard_map/ppermute | solution.py:243
  22.2 0.8 collective-permute-done
  23.0 0.1 fusion.3
  23.0 10.6 %collective-permute-start.1 = (f32[16,4]{1,0:T(8,128)S(1)}, f32[16,4]{1,0:T(8,128)S(1)}, u32[]{:S(2)}, u32[]{:S(2)}) collective-permute-start(f32[16,4]{1,0:T(8,128)S(1)} %fusion.3), channel_id=1, source_target_pairs={{0,16},{2,18},{4,20},{6,22},{8,24},{10,26},{12,28},{14,30},{16,0},... | collective-permute-start | bytes 776 | tf_op jit(solution)/shard_map/ppermute | solution.py:243
  33.7 1.0 collective-permute-done.1
  34.7 0.1 fusion.4
  34.8 3.1 %collective-permute-start.2 = (f32[16,4]{1,0:T(8,128)S(1)}, f32[16,4]{1,0:T(8,128)S(1)}, u32[]{:S(2)}, u32[]{:S(2)}) collective-permute-start(f32[16,4]{1,0:T(8,128)S(1)} %fusion.4), channel_id=1, source_target_pairs={{0,4},{2,6},{4,0},{6,2},{8,12},{10,14},{12,8},{14,10},{16,20},{18,... | collective-permute-start | bytes 776 | tf_op jit(solution)/shard_map/ppermute | solution.py:243
  37.9 0.6 pad_add_fusion.place
  38.5 0.6 collective-permute-done.2
  39.2 4.4 %collective-permute-start.3 = (f32[16,4]{1,0:T(8,128)S(1)}, f32[16,4]{1,0:T(8,128)S(1)}, u32[]{:S(2)}, u32[]{:S(2)}) collective-permute-start(f32[16,4]{1,0:T(8,128)S(1)} %add.24), channel_id=1, source_target_pairs={{0,8},{2,10},{4,12},{6,14},{8,0},{10,2},{12,4},{14,6},{16,24},{18,... | collective-permute-start | bytes 776 | tf_op jit(solution)/shard_map/ppermute | solution.py:243
  43.5 0.0 copy-done.5
  43.5 0.7 copy.19
  44.2 0.7 copy-done.6
  44.9 0.7 copy.18.sum_views
  45.6 0.0 collective-permute-done.3
  45.6 0.6 add.25.table
  46.2 0.0 collective-permute-done.5.right_kv
  46.2 0.0 collective-permute-done.4.left_kv
  46.2 0.0 all-to-all-done.sums
  46.2 7.4 %attention.1 = (bf16[128,1024]{1,0:T(8,128)(2,1)}, bf16[128,1024]{1,0:T(8,128)(2,1)}, bf16[128,2048]{1,0:T(8,128)(2,1)}, bf16[128,2048]{1,0:T(8,128)(2,1)}, f32[...) custom-call(s32[2]{0:T(128)} %pad_add_fusion.place, ...), custom_call_target="tpu_custom_call" | custom-call | tf_op jit(solution)/shard_map/attention/pallas_call | solution.py:254
  53.7 3.3 %collective-permute-start.6 = (bf16[128,2048]{1,0:T(8,128)(2,1)}, bf16[128,2048]{1,0:T(8,128)(2,1)S(1)}, u32[]{:S(2)}, u32[]{:S(2)}) collective-permute-start(bf16[128,2048]{1,0:T(8,128)(2,1)} %get-tuple-element.21), channel_id=1, source_target_pairs={{0,32},{32,64},{64,96},{96,128},{128,160},{160,192},{192,224},{224... | collective-permute-start | bytes 1572872 | tf_op jit(solution)/shard_map/ppermute | solution.py:286
  57.0 1.3 %collective-permute-start.7 = (bf16[128,2048]{1,0:T(8,128)(2,1)}, bf16[128,2048]{1,0:T(8,128)(2,1)S(1)}, u32[]{:S(2)}, u32[]{:S(2)}) collective-permute-start(bf16[128,2048]{1,0:T(8,128)(2,1)} %get-tuple-element.22), channel_id=1, source_target_pairs={{32,0},{64,32},{96,64},{128,96},{160,128},{192,160},{224,192},{256... | collective-permute-start | bytes 1572872 | tf_op jit(solution)/shard_map/ppermute | solution.py:285
  58.3 10.2 %collective-permute-start.8 = (bf16[8,128,128]{2,1,0:T(8,128)(2,1)}, bf16[8,128,128]{2,1,0:T(8,128)(2,1)S(1)}, u32[]{:S(2)}, u32[]{:S(2)}) collective-permute-start(bf16[8,128,128]{2,1,0:T(8,128)(2,1)} %get-tuple-element.24), channel_id=1, source_target_pairs={{0,256},{256,0},{1,257},{257,1},{2,258},{258,2},{3,259},{259,3},{4... | collective-permute-start | bytes 786440 | tf_op jit(solution)/shard_map/ppermute | solution.py:283
  68.5 20.4 %all_to_all.15.bias_part = f32[64,1,128]{2,1,0:T(1,128)S(1)} all-to-all(f32[64,1,128]{2,1,0:T(1,128)} %get-tuple-element.25), channel_id=1, replica_groups=mesh['half'=2,'y'=8,'fsdp'=16,'dp'=2] {'half','fsdp','dp'}, dimensions={0} | all-to-all | bytes 65536 | tf_op jit(solution)/shard_map/all_to_all | solution.py:284
  88.9 0.0 collective-permute-done.8.far
  88.9 1.0 copy-done
  89.9 0.8 merge.1
  90.8 3.4 %all-to-all-start.2 = ((bf16[8,136,128]{2,1,0:T(8,128)(2,1)}), bf16[8,136,128]{2,1,0:T(8,128)(2,1)S(1)}, u32[]{:S(2)}, u32[]{:S(2)}) async-start(bf16[8,136,128]{2,1,0:T(8,128)(2,1)} %merge.1), calls=%async_computation.2 | async-start | bytes 557056 | tf_op jit(solution)/shard_map/all_to_all | solution.py:295
  94.2 0.0 collective-permute-done.6
  94.2 0.0 collective-permute-done.7
  94.2 0.0 copy-done.1
  94.2 0.2 convert_add_fusion
  94.4 0.7 fusion.2
  95.2 0.8 fusion.1
  95.9 9.3 %all-to-all-done.2.terms = bf16[8,136,128]{2,1,0:T(8,128)(2,1)S(1)} async-done(((bf16[8,136,128]{2,1,0:T(8,128)(2,1)}), bf16[8,136,128]{2,1,0:T(8,128)(2,1)S(1)}, u32[]{:S(2)}, u32[]{:S(2)}) %all-to-all-start.2) | async-done | bytes 278560 | tf_op jit(solution)/shard_map/all_to_all | solution.py:295
  105.2 0.6 finish.1
  (7 shorter events, 0.1 us)
Async XLA Ops:
  2.2 10.3 %copy-start.2 = (bf16[1,128,1024]{2,1,0:T(8,128)(2,1)S(1)}, bf16[1,128,1024]{2,1,0:T(8,128)(2,1)}, u32[]{:S(2)}) copy-start(bf16[1,128,1024]{2,1,0:T(8,128)(2,1)} %param.12) | copy-start | bytes 786436
  2.2 10.4 %copy-start.3 = (bf16[1,128,1024]{2,1,0:T(8,128)(2,1)S(1)}, bf16[1,128,1024]{2,1,0:T(8,128)(2,1)}, u32[]{:S(2)}) copy-start(bf16[1,128,1024]{2,1,0:T(8,128)(2,1)} %param.11) | copy-start | bytes 786436
  2.2 44.0 %all-to-all-start = ((bf16[16,16,1024]{2,1,0:T(8,128)(2,1)}), bf16[16,16,1024]{2,1,0:T(8,128)(2,1)S(1)}, u32[]{:S(2)}, u32[]{:S(2)}) async-start(bf16[16,16,1024]{2,1,0:T(8,128)(2,1)} %broadcast_in_dim.41), calls=%async_computation | async-start | bytes 1048576 | tf_op jit(solution)/shard_map/all_to_all | solution.py:237
  12.6 33.6 %collective-permute-start.5 = (bf16[128,2048]{1,0:T(8,128)(2,1)S(1)}, bf16[128,2048]{1,0:T(8,128)(2,1)S(1)}, u32[]{:S(2)}, u32[]{:S(2)}) collective-permute-start(bf16[128,2048]{1,0:T(8,128)(2,1)S(1)} %pad_maximum_fusion.own_kv), channel_id=1, source_target_pairs={{32,0},{64,32},{96,64},{128,96},{160,128},{192,160},{224,192},{256... | collective-permute-start | bytes 1572872 | tf_op jit(solution)/shard_map/ppermute | solution.py:234
  13.9 32.3 %collective-permute-start.4 = (bf16[128,2048]{1,0:T(8,128)(2,1)S(1)}, bf16[128,2048]{1,0:T(8,128)(2,1)S(1)}, u32[]{:S(2)}, u32[]{:S(2)}) collective-permute-start(bf16[128,2048]{1,0:T(8,128)(2,1)S(1)} %pad_maximum_fusion.own_kv), channel_id=1, source_target_pairs={{0,32},{32,64},{64,96},{96,128},{128,160},{160,192},{192,224},{224... | collective-permute-start | bytes 1572872 | tf_op jit(solution)/shard_map/ppermute | solution.py:233
  18.0 0.7 copy-start.4
  18.7 4.2 %collective-permute-start = (f32[16,4]{1,0:T(8,128)S(1)}, f32[16,4]{1,0:T(8,128)S(1)}, u32[]{:S(2)}, u32[]{:S(2)}) collective-permute-start(f32[16,4]{1,0:T(8,128)S(1)} %broadcast_select_fusion), channel_id=1, source_target_pairs={{0,2},{2,0},{4,6},{6,4},{8,10},{10,8},{12,14},{14,12},{16,18},{18,... | collective-permute-start | bytes 776 | tf_op jit(solution)/shard_map/ppermute | solution.py:243
  23.0 11.7 %collective-permute-start.1 = (f32[16,4]{1,0:T(8,128)S(1)}, f32[16,4]{1,0:T(8,128)S(1)}, u32[]{:S(2)}, u32[]{:S(2)}) collective-permute-start(f32[16,4]{1,0:T(8,128)S(1)} %fusion.3), channel_id=1, source_target_pairs={{0,16},{2,18},{4,20},{6,22},{8,24},{10,26},{12,28},{14,30},{16,0},... | collective-permute-start | bytes 776 | tf_op jit(solution)/shard_map/ppermute | solution.py:243
  34.8 4.4 %collective-permute-start.2 = (f32[16,4]{1,0:T(8,128)S(1)}, f32[16,4]{1,0:T(8,128)S(1)}, u32[]{:S(2)}, u32[]{:S(2)}) collective-permute-start(f32[16,4]{1,0:T(8,128)S(1)} %fusion.4), channel_id=1, source_target_pairs={{0,4},{2,6},{4,0},{6,2},{8,12},{10,14},{12,8},{14,10},{16,20},{18,... | collective-permute-start | bytes 776 | tf_op jit(solution)/shard_map/ppermute | solution.py:243
  38.5 5.0 %copy-start.5 = (s32[1,16,3]{1,0,2:T(1,128)S(1)}, s32[1,16,3]{1,0,2:T(1,128)}, u32[]{:S(2)}) copy-start(s32[1,16,3]{1,0,2:T(1,128)} %param.17) | copy-start | bytes 580
  39.2 6.5 %collective-permute-start.3 = (f32[16,4]{1,0:T(8,128)S(1)}, f32[16,4]{1,0:T(8,128)S(1)}, u32[]{:S(2)}, u32[]{:S(2)}) collective-permute-start(f32[16,4]{1,0:T(8,128)S(1)} %add.24), channel_id=1, source_target_pairs={{0,8},{2,10},{4,12},{6,14},{8,0},{10,2},{12,4},{14,6},{16,24},{18,... | collective-permute-start | bytes 776 | tf_op jit(solution)/shard_map/ppermute | solution.py:243
  44.2 0.7 copy-start.6
  53.7 40.5 %collective-permute-start.6 = (bf16[128,2048]{1,0:T(8,128)(2,1)}, bf16[128,2048]{1,0:T(8,128)(2,1)S(1)}, u32[]{:S(2)}, u32[]{:S(2)}) collective-permute-start(bf16[128,2048]{1,0:T(8,128)(2,1)} %get-tuple-element.21), channel_id=1, source_target_pairs={{0,32},{32,64},{64,96},{96,128},{128,160},{160,192},{192,224},{224... | collective-permute-start | bytes 1572872 | tf_op jit(solution)/shard_map/ppermute | solution.py:286
  57.0 37.2 %collective-permute-start.7 = (bf16[128,2048]{1,0:T(8,128)(2,1)}, bf16[128,2048]{1,0:T(8,128)(2,1)S(1)}, u32[]{:S(2)}, u32[]{:S(2)}) collective-permute-start(bf16[128,2048]{1,0:T(8,128)(2,1)} %get-tuple-element.22), channel_id=1, source_target_pairs={{32,0},{64,32},{96,64},{128,96},{160,128},{192,160},{224,192},{256... | collective-permute-start | bytes 1572872 | tf_op jit(solution)/shard_map/ppermute | solution.py:285
  58.3 30.6 %collective-permute-start.8 = (bf16[8,128,128]{2,1,0:T(8,128)(2,1)}, bf16[8,128,128]{2,1,0:T(8,128)(2,1)S(1)}, u32[]{:S(2)}, u32[]{:S(2)}) collective-permute-start(bf16[8,128,128]{2,1,0:T(8,128)(2,1)} %get-tuple-element.24), channel_id=1, source_target_pairs={{0,256},{256,0},{1,257},{257,1},{2,258},{258,2},{3,259},{259,3},{4... | collective-permute-start | bytes 786440 | tf_op jit(solution)/shard_map/ppermute | solution.py:283
  88.9 1.0 copy-start
  89.9 4.3 %copy-start.1 = (f32[128,2048]{1,0:T(8,128)S(1)}, f32[128,2048]{1,0:T(8,128)}, u32[]{:S(2)}) copy-start(f32[128,2048]{1,0:T(8,128)} %get-tuple-element.20) | copy-start | bytes 3145732
  90.8 14.4 %all-to-all-start.2 = ((bf16[8,136,128]{2,1,0:T(8,128)(2,1)}), bf16[8,136,128]{2,1,0:T(8,128)(2,1)S(1)}, u32[]{:S(2)}, u32[]{:S(2)}) async-start(bf16[8,136,128]{2,1,0:T(8,128)(2,1)} %merge.1), calls=%async_computation.2 | async-start | bytes 557056 | tf_op jit(solution)/shard_map/all_to_all | solution.py:295
